TPU v7x, 32 devices: a whole 2x2x4 slice. The times are simulated.
32 devices in a mesh: dp: 8 (over z, x), ctx: 2 (over y), tp: 2 (over core).
Axes of the slice: x: 2, y: 2, z: 4, core: 2. Of those that a mesh axis runs over, the one named last changes fastest.
Arguments:
- tokens: bfloat16 [16, 1024, 768], P('dp', 'ctx'), may hold values from -6 to 6
- lengths: int32 [16], P('dp'), may hold values from 256 to 1024, as said below
- ln1_gain: float32 [768], P('dp'), may hold values from 0.5 to 1.5
- ln1_bias: float32 [768], P('dp'), may hold values from -1.75 to 1.75
- w_qkv: bfloat16 [768, 3, 768], P('dp', None, 'tp'), may hold values from -0.21875 to 0.21875
- qv_bias: float32 [384, 2, 2], P('dp', None, 'tp'), may hold values from -1.25 to 1.25
- w_out: bfloat16 [768, 768], P('dp', 'tp'), may hold values from -1.75 to 1.75
- out_bias: float32 [768], P('dp'), may hold values from -1.75 to 1.75
- ln2_gain: float32 [768], P('dp'), may hold values from 0.5 to 1.5
- ln2_bias: float32 [768], P('dp'), may hold values from -1.75 to 1.75
- w_fc: bfloat16 [768, 3072], P('dp', 'tp'), may hold values from -0.21875 to 0.21875
- fc_bias: float32 [1536, 2], P('dp', 'tp'), may hold values from -1.75 to 1.75
- w_proj: bfloat16 [768, 3072], P('dp', 'tp'), may hold values from -0.21875 to 0.21875
- proj_bias: float32 [768], P('dp'), may hold values from -1.75 to 1.75
- cotangent: bfloat16 [16, 1024, 768], P('dp', 'ctx'), may hold values from -6 to 6
Outputs:
- output: bfloat16 [16, 1024, 768], P('dp', 'ctx')
- grad_tokens: bfloat16 [16, 1024, 768], P('dp', 'ctx')
- grad_ln1_gain: float32 [768], P('dp')
- grad_ln1_bias: float32 [768], P('dp')
- grad_w_qkv: float32 [768, 3, 768], P('dp', None, 'tp')
- grad_qv_bias: float32 [384, 2, 2], P('dp', None, 'tp')
- grad_w_out: float32 [768, 768], P('dp', 'tp')
- grad_out_bias: float32 [768], P('dp')
- grad_ln2_gain: float32 [768], P('dp')
- grad_ln2_bias: float32 [768], P('dp')
- grad_w_fc: float32 [768, 3072], P('dp', 'tp')
- grad_fc_bias: float32 [1536, 2], P('dp', 'tp')
- grad_w_proj: float32 [768, 3072], P('dp', 'tp')
- grad_proj_bias: float32 [768], P('dp')
Inputs may be any that keep to these rules, and one draw needn't show every extreme that they name: lengths[s] is the number of valid slots of sequence s; slots from lengths[s] on are padding.
All inputs are finite; a program needn't handle non-finite values.
Results may differ from a plain program's by a relative error of at most 0.03.
Values may be sent and summed in bfloat16 or wider, within the bound.
A program may use at most 192 MiB of HBM per device.

v0:
```python
import jax
import jax.numpy as jnp
from jax import lax
from jax.sharding import PartitionSpec as P

HD = 64


epsilon = 1e-05
masked_score = -1e30
gelu_factor = 1.702


def apply_layer_norm(row_values, gain_vec, shift_vec):
    centred = row_values - jnp.mean(row_values, axis=-1, keepdims=True)
    inv_std = lax.rsqrt(jnp.mean(centred * centred, axis=-1, keepdims=True) + epsilon)
    normed = centred * inv_std
    return (normed * gain_vec + shift_vec, normed, inv_std)


def layer_norm_back(grad_norm_out, normed, inv_std, gain_vec):
    scaled = grad_norm_out * gain_vec
    grad_in = inv_std * (
        scaled
        - jnp.mean(scaled, axis=-1, keepdims=True)
        - normed * jnp.mean(scaled * normed, axis=-1, keepdims=True)
    )
    return (
        grad_in,
        jnp.sum(grad_norm_out * normed, axis=(0, 1)),
        jnp.sum(grad_norm_out, axis=(0, 1)),
    )


def tensor_sum(partial_sum):
    return lax.psum(partial_sum.astype(jnp.bfloat16), "tp").astype(jnp.float32)


def masked_scores(query_rows, key_rows, length):
    key_count = key_rows.shape[0]
    key_heads = key_rows.reshape(key_count, query_rows.shape[1], HD)
    scores = jnp.einsum(
        "qhe,khe->hqk", query_rows, key_heads, preferred_element_type=jnp.float32
    ) * HD ** (-0.5)
    valid_keys = jnp.arange(key_count) < length
    return (jnp.where(valid_keys[None, None, :], scores, masked_score), key_heads)


def attend_one(packed):
    query_rows, key_rows, value_rows, length = packed
    scores, key_heads = masked_scores(query_rows, key_rows, length)
    row_peak = jnp.max(scores, axis=-1, keepdims=True)
    raised = jnp.exp(scores - row_peak)
    row_total = jnp.sum(raised, axis=-1, keepdims=True)
    prob_low = (raised / row_total).astype(jnp.bfloat16)
    value_heads = value_rows.reshape(value_rows.shape[0], query_rows.shape[1], HD)
    mixed_rows = jnp.einsum(
        "hqk,khe->qhe", prob_low, value_heads, preferred_element_type=jnp.float32
    )
    log_total = (row_peak + jnp.log(row_total))[..., 0]
    return (mixed_rows.reshape(query_rows.shape[0], -1).astype(jnp.bfloat16), log_total)


def attend_back_one(packed):
    query_rows, key_rows, value_rows, length, log_total, grad_mixed = packed
    head_count = query_rows.shape[1]
    scores, key_heads = masked_scores(query_rows, key_rows, length)
    value_heads = value_rows.reshape(value_rows.shape[0], head_count, HD)
    grad_heads = grad_mixed.reshape(grad_mixed.shape[0], head_count, HD)
    prob_full = jnp.exp(scores - log_total[..., None])
    prob_low = prob_full.astype(jnp.bfloat16)
    grad_values = jnp.einsum(
        "hqk,qhe->khe", prob_low, grad_heads, preferred_element_type=jnp.float32
    )
    grad_probs = jnp.einsum(
        "qhe,khe->hqk", grad_heads, value_heads, preferred_element_type=jnp.float32
    )
    inner_sum = jnp.sum(grad_probs * prob_full, axis=-1, keepdims=True)
    grad_scores = (prob_full * (grad_probs - inner_sum)).astype(jnp.bfloat16)
    score_scale = HD ** (-0.5)
    grad_query = (
        jnp.einsum("hqk,khe->qhe", grad_scores, key_heads, preferred_element_type=jnp.float32)
        * score_scale
    )
    grad_keys = (
        jnp.einsum("hqk,qhe->khe", grad_scores, query_rows, preferred_element_type=jnp.float32)
        * score_scale
    )
    key_count = key_rows.shape[0]
    return (
        grad_query.reshape(query_rows.shape[0], -1),
        grad_keys.reshape(key_count, -1),
        grad_values.reshape(key_count, -1),
    )


def on_device(
    tokens,
    lengths,
    ln1_gain,
    ln1_bias,
    w_qkv,
    qv_bias,
    w_out,
    out_bias,
    ln2_gain,
    ln2_bias,
    w_fc,
    fc_bias,
    w_proj,
    proj_bias,
    cotangent,
):
    (
        first_norm_gain,
        first_norm_shift,
        complete_query_key_value,
        full_qv_bias,
        complete_output_weight,
        full_out_bias,
        second_norm_gain,
        second_norm_shift,
        complete_expand_weight,
        full_fc_bias,
        complete_projection_weight,
        full_proj_bias,
    ) = (
        lax.all_gather(ln1_gain.astype(jnp.bfloat16), "dp", axis=0, tiled=True).astype(
            ln1_gain.dtype
        ),
        lax.all_gather(ln1_bias.astype(jnp.bfloat16), "dp", axis=0, tiled=True).astype(
            ln1_bias.dtype
        ),
        lax.all_gather(w_qkv, "dp", axis=0, tiled=True),
        lax.all_gather(qv_bias.astype(jnp.bfloat16), "dp", axis=0, tiled=True).astype(
            qv_bias.dtype
        ),
        lax.all_gather(w_out, "dp", axis=0, tiled=True),
        lax.all_gather(out_bias.astype(jnp.bfloat16), "dp", axis=0, tiled=True).astype(
            out_bias.dtype
        ),
        lax.all_gather(ln2_gain.astype(jnp.bfloat16), "dp", axis=0, tiled=True).astype(
            ln2_gain.dtype
        ),
        lax.all_gather(ln2_bias.astype(jnp.bfloat16), "dp", axis=0, tiled=True).astype(
            ln2_bias.dtype
        ),
        lax.all_gather(w_fc, "dp", axis=0, tiled=True),
        lax.all_gather(fc_bias.astype(jnp.bfloat16), "dp", axis=0, tiled=True).astype(
            fc_bias.dtype
        ),
        lax.all_gather(w_proj, "dp", axis=0, tiled=True),
        lax.all_gather(proj_bias.astype(jnp.bfloat16), "dp", axis=0, tiled=True).astype(
            proj_bias.dtype
        ),
    )
    seq_count, local_rows, model_width = tokens.shape
    head_count = complete_query_key_value.shape[2] // HD
    residual_input = tokens.astype(jnp.float32)
    first_normalized_rows, first_centered_scaled, first_inverse_deviation = apply_layer_norm(
        residual_input, first_norm_gain, first_norm_shift
    )
    first_hidden_rows = first_normalized_rows.astype(jnp.bfloat16)
    projected = jnp.einsum(
        "ynj,jrq->ynrq",
        first_hidden_rows,
        complete_query_key_value,
        preferred_element_type=jnp.float32,
    )
    query_low = (projected[:, :, 0] + full_qv_bias[:, 0, 0]).astype(jnp.bfloat16)
    key_low = projected[:, :, 1].astype(jnp.bfloat16)
    value_low = (projected[:, :, 2] + full_qv_bias[:, 1, 0]).astype(jnp.bfloat16)
    all_keys, all_values = (
        lax.all_gather(key_low, "ctx", axis=1, tiled=True),
        lax.all_gather(value_low, "ctx", axis=1, tiled=True),
    )
    query_heads = query_low.reshape(seq_count, local_rows, head_count, HD)
    attention_mixed_narrow, log_total = lax.map(
        attend_one, (query_heads, all_keys, all_values, lengths)
    )
    attn_partial = jnp.einsum(
        "paj,yj->pay",
        attention_mixed_narrow,
        complete_output_weight,
        preferred_element_type=jnp.float32,
    )
    residual_middle = residual_input + tensor_sum(attn_partial) + full_out_bias
    second_normalized_rows, second_centered_scaled, second_inverse_deviation = apply_layer_norm(
        residual_middle, second_norm_gain, second_norm_shift
    )
    second_hidden_rows = second_normalized_rows.astype(jnp.bfloat16)
    pre_act = (
        jnp.einsum(
            "icg,gh->ich",
            second_hidden_rows,
            complete_expand_weight,
            preferred_element_type=jnp.float32,
        )
        + full_fc_bias[:, 0]
    )
    gate_sig = jax.nn.sigmoid(gelu_factor * pre_act)
    activation_narrow = (pre_act * gate_sig).astype(jnp.bfloat16)
    perceptron_partial_output = jnp.einsum(
        "pvn,jn->pvj",
        activation_narrow,
        complete_projection_weight,
        preferred_element_type=jnp.float32,
    )
    output = residual_middle + tensor_sum(perceptron_partial_output) + full_proj_bias
    slot_index = lax.axis_index("ctx") * local_rows + jnp.arange(local_rows)
    live_rows = (slot_index[None, :] < lengths[:, None])[..., None]
    narrow_gradient = jnp.where(live_rows, cotangent, jnp.zeros_like(cotangent))
    grad_top = narrow_gradient.astype(jnp.float32)
    activation_gradient = jnp.einsum(
        "icg,gh->ich",
        narrow_gradient,
        complete_projection_weight,
        preferred_element_type=jnp.float32,
    )
    gelu_slope = gate_sig * (1.0 + gelu_factor * pre_act * (1.0 - gate_sig))
    preactivation_gradient = (activation_gradient * gelu_slope).astype(jnp.bfloat16)
    projection_weight_gradient = jnp.einsum(
        "pjh,pjq->hq", narrow_gradient, activation_narrow, preferred_element_type=jnp.float32
    )
    grad_proj_b = jnp.sum(grad_top, axis=(0, 1))
    expand_weight_gradient = jnp.einsum(
        "pjh,pjq->hq",
        second_hidden_rows,
        preactivation_gradient,
        preferred_element_type=jnp.float32,
    )
    grad_fc_b = jnp.sum(preactivation_gradient, axis=(0, 1), dtype=jnp.float32)
    second_hidden_gradient = tensor_sum(
        jnp.einsum(
            "pvn,jn->pvj",
            preactivation_gradient,
            complete_expand_weight,
            preferred_element_type=jnp.float32,
        )
    )
    grad_norm_two, grad_gain_two, grad_shift_two = layer_norm_back(
        second_hidden_gradient, second_centered_scaled, second_inverse_deviation, second_norm_gain
    )
    grad_mid = grad_top + grad_norm_two
    middle_narrow_gradient = grad_mid.astype(jnp.bfloat16)
    grad_out_w = jnp.einsum(
        "ahk,ahb->kb",
        middle_narrow_gradient,
        attention_mixed_narrow,
        preferred_element_type=jnp.float32,
    )
    grad_out_b = jnp.sum(grad_mid, axis=(0, 1))
    grad_mixed = jnp.einsum(
        "fok,kg->fog",
        middle_narrow_gradient,
        complete_output_weight,
        preferred_element_type=jnp.float32,
    ).astype(jnp.bfloat16)
    back_keys, back_values = (
        lax.all_gather(key_low, "ctx", axis=1, tiled=True),
        lax.all_gather(value_low, "ctx", axis=1, tiled=True),
    )
    grad_query, grad_keys_part, grad_values_part = lax.map(
        attend_back_one, (query_heads, back_keys, back_values, lengths, log_total, grad_mixed)
    )
    grad_keys, grad_values = (
        lax.psum_scatter(
            grad_keys_part.astype(jnp.bfloat16), "ctx", scatter_dimension=1, tiled=True
        ).astype(jnp.float32),
        lax.psum_scatter(
            grad_values_part.astype(jnp.bfloat16), "ctx", scatter_dimension=1, tiled=True
        ).astype(jnp.float32),
    )
    grad_q_low = grad_query.astype(jnp.bfloat16)
    grad_k_low = grad_keys.astype(jnp.bfloat16)
    grad_v_low = grad_values.astype(jnp.bfloat16)
    query_key_value_gradient = jnp.stack([grad_q_low, grad_k_low, grad_v_low], axis=2)
    grad_qkv_w = jnp.einsum(
        "gav,gazy->vzy",
        first_hidden_rows,
        query_key_value_gradient,
        preferred_element_type=jnp.float32,
    )
    grad_qv_b = jnp.stack(
        [
            jnp.sum(grad_q_low, axis=(0, 1), dtype=jnp.float32),
            jnp.sum(grad_v_low, axis=(0, 1), dtype=jnp.float32),
        ],
        axis=1,
    )[:, :, None]
    first_hidden_gradient = tensor_sum(
        jnp.einsum(
            "qkbf,nbf->qkn",
            query_key_value_gradient,
            complete_query_key_value,
            preferred_element_type=jnp.float32,
        )
    )
    grad_norm_one, grad_gain_one, grad_shift_one = layer_norm_back(
        first_hidden_gradient, first_centered_scaled, first_inverse_deviation, first_norm_gain
    )
    grad_tokens = (grad_mid + grad_norm_one).astype(jnp.bfloat16)
    grad_list = (
        grad_gain_one,
        grad_shift_one,
        grad_qkv_w,
        grad_qv_b,
        grad_out_w,
        grad_out_b,
        grad_gain_two,
        grad_shift_two,
        expand_weight_gradient,
        grad_fc_b[:, None],
        projection_weight_gradient,
        grad_proj_b,
    )
    shard_list = (
        lax.psum_scatter(grad_list[0], "dp", scatter_dimension=0, tiled=True),
        lax.psum_scatter(grad_list[1], "dp", scatter_dimension=0, tiled=True),
        lax.psum_scatter(grad_list[2], "dp", scatter_dimension=0, tiled=True),
        lax.psum_scatter(grad_list[3], "dp", scatter_dimension=0, tiled=True),
        lax.psum_scatter(grad_list[4], "dp", scatter_dimension=0, tiled=True),
        lax.psum_scatter(grad_list[5], "dp", scatter_dimension=0, tiled=True),
        lax.psum_scatter(grad_list[6], "dp", scatter_dimension=0, tiled=True),
        lax.psum_scatter(grad_list[7], "dp", scatter_dimension=0, tiled=True),
        lax.psum_scatter(grad_list[8], "dp", scatter_dimension=0, tiled=True),
        lax.psum_scatter(grad_list[9], "dp", scatter_dimension=0, tiled=True),
        lax.psum_scatter(grad_list[10], "dp", scatter_dimension=0, tiled=True),
        lax.psum_scatter(grad_list[11], "dp", scatter_dimension=0, tiled=True),
    )
    summed = (
        lax.psum(shard_list[0].astype(jnp.bfloat16), "ctx").astype(jnp.float32),
        lax.psum(shard_list[1].astype(jnp.bfloat16), "ctx").astype(jnp.float32),
        lax.psum(shard_list[2].astype(jnp.bfloat16), "ctx").astype(jnp.float32),
        lax.psum(shard_list[3].astype(jnp.bfloat16), "ctx").astype(jnp.float32),
        lax.psum(shard_list[4].astype(jnp.bfloat16), "ctx").astype(jnp.float32),
        lax.psum(shard_list[5].astype(jnp.bfloat16), "ctx").astype(jnp.float32),
        lax.psum(shard_list[6].astype(jnp.bfloat16), "ctx").astype(jnp.float32),
        lax.psum(shard_list[7].astype(jnp.bfloat16), "ctx").astype(jnp.float32),
        lax.psum(shard_list[8].astype(jnp.bfloat16), "ctx").astype(jnp.float32),
        lax.psum(shard_list[9].astype(jnp.bfloat16), "ctx").astype(jnp.float32),
        lax.psum(shard_list[10].astype(jnp.bfloat16), "ctx").astype(jnp.float32),
        lax.psum(shard_list[11].astype(jnp.bfloat16), "ctx").astype(jnp.float32),
    )
    return (output.astype(jnp.bfloat16), grad_tokens) + tuple(summed)


def solution(mesh):
    return jax.shard_map(
        on_device,
        mesh=mesh,
        in_specs=(
            P("dp", "ctx", None),
            P("dp"),
            P("dp"),
            P("dp"),
            P("dp", None, "tp"),
            P("dp", None, "tp"),
            P("dp", "tp"),
            P("dp"),
            P("dp"),
            P("dp"),
            P("dp", "tp"),
            P("dp", "tp"),
            P("dp", "tp"),
            P("dp"),
            P("dp", "ctx", None),
        ),
        out_specs=(
            P("dp", "ctx", None),
            P("dp", "ctx", None),
            P("dp"),
            P("dp"),
            P("dp", None, "tp"),
            P("dp", None, "tp"),
            P("dp", "tp"),
            P("dp"),
            P("dp"),
            P("dp"),
            P("dp", "tp"),
            P("dp", "tp"),
            P("dp", "tp"),
            P("dp"),
        ),
        check_vma=False,
    )
```

profile of v0, /device:TPU:0, one launch (start us, length us, event | category | flops | bytes accessed | tf_op | source)
XLA Modules:
  0.0 1045.6 jit_solution(10935551577769834160)
XLA Ops:
  17.4 39.9 %all-reduce.14 = (bf16[768]{0:T(1024)(128)(2,1)S(1)}, bf16[768]{0:T(1024)(128)(2,1)S(1)}, bf16[768]{0:T(1024)(128)(2,1)S(1)}, bf16[768]{0:T(1024)(128)(2,1)S(1)}...) all-reduce(bf16[768]{0:T(1024)(128)(2,1)S(1)} %dynamic-update-slice, ...), channel_id=1, replica_groups=mesh['dp'=8,'ctx'=2,'tp'=2] {'dp'}, use_global_device_ids=true, to_apply=%add.4 | all-reduce | flops 6144 | bytes 24576
  57.4 30.6 %all_gather.47 = bf16[384,2,1]{2,1,0:T(2,128)(2,1)S(1)} all-gather(bf16[48,2,1]{2,1,0:T(2,128)(2,1)S(1)} %copy.65), channel_id=1, replica_groups=mesh['dp'=8,'ctx'=2,'tp'=2] {'dp'}, dimensions={0}, use_global_device_ids=true | all-gather | bytes 1728 | tf_op jit(solution)/shard_map/all_gather | solution.py:135
  92.7 3.9 fusion.55
  99.8 2.4 slice.34
  102.4 31.5 %all_gather.50 = bf16[768,384]{1,0:T(8,128)(2,1)S(1)} all-gather(bf16[96,384]{1,0:T(8,128)(2,1)S(1)} %copy-done.23), channel_id=1, replica_groups=mesh['dp'=8,'ctx'=2,'tp'=2] {'dp'}, dimensions={0}, use_global_device_ids=true | all-gather | bytes 663552 | tf_op jit(solution)/shard_map/all_gather | solution.py:138
  135.6 18.1 %all-gather.15.cloned.1.call-done = bf16[2,1024,1,384]{1,3,2,0:T(8,128)(2,1)} async-done(((bf16[2,512,1,384]{1,3,2,0:T(8,128)(2,1)}), bf16[2,1024,1,384]{1,3,2,0:T(8,128)(2,1)}) %all-gather.15.cloned.1.call-update) | async-done | bytes 1572880 | tf_op jit(solution)/shard_map/all_gather | solution.py:174
  153.7 26.6 %while.26 = (s32[]{:T(128)}, bf16[2,512,384]{1,2,0:T(8,128)(2,1)}, f32[2,6,512]{2,1,0:T(8,128)S(1)}, bf16[2,1024,384]{1,2,0:T(8,128)(2,1)}, s32[2]{0:T(128)}, /*...) while((s32[]{:T(128)}, bf16[2,512,384]{1,2,0:T(8,128)(2,1)}, ...), condition=%wide.region_5.6_spmd, body=%wide.region_2.5_spmd.sunk | while | flops 843249664 | bytes 50446516 | solution.py:178
  159.1 3.0 fusion.116
  162.1 3.9 fusion.117
  172.4 3.0 fusion.116
  175.5 3.9 fusion.117
  180.4 3.3 convolution_convert_fusion
  186.0 18.2 %all-reduce.23.cloned.1.call-done = bf16[2,512,768]{2,1,0:T(8,128)(2,1)} async-done(((bf16[2,512,768]{2,1,0:T(8,128)(2,1)}), bf16[2,512,768]{2,1,0:T(8,128)(2,1)}) %all-reduce.23.cloned.1.call-update) | async-done | bytes 1572880 | tf_op jit(solution)/shard_map/psum | solution.py:36
  207.2 52.0 %all-gather.11.cloned.1.call-done = bf16[768,1536]{1,0:T(8,128)(2,1)} async-done(((bf16[96,1536]{1,0:T(8,128)(2,1)}), bf16[768,1536]{1,0:T(8,128)(2,1)}) %all-gather.11.cloned.1.call-update) | async-done | bytes 2359312 | tf_op jit(solution)/shard_map/all_gather | solution.py:148
  259.3 9.3 multiply_convert_fusion.2
  268.6 43.1 %all-gather.13.cloned.1.call-done = bf16[768,1536]{1,0:T(8,128)(2,1)} async-done(((bf16[96,1536]{1,0:T(8,128)(2,1)}), bf16[768,1536]{1,0:T(8,128)(2,1)}) %all-gather.13.cloned.1.call-update) | async-done | bytes 2359312 | tf_op jit(solution)/shard_map/all_gather | solution.py:152
  311.7 8.0 convert_reduce_fusion
  321.3 3.7 fusion.57
  325.6 18.5 %all-reduce.25.cloned.1.call-done = bf16[2,512,768]{2,1,0:T(8,128)(2,1)} async-done(((bf16[2,512,768]{2,1,0:T(8,128)(2,1)}), bf16[2,512,768]{2,1,0:T(8,128)(2,1)}) %all-reduce.25.cloned.1.call-update) | async-done | bytes 1572880 | tf_op jit(solution)/shard_map/psum | solution.py:36
  344.1 4.0 fusion.45
  348.2 2.7 fusion.79
  354.5 75.3 %while.27 = (s32[]{:T(128)}, bf16[2,512,384]{2,1,0:T(8,128)(2,1)}, bf16[2,1024,384]{2,1,0:T(8,128)(2,1)}, bf16[2,1024,384]{2,1,0:T(8,128)(2,1)}, bf16[2,1024,384...) while((s32[]{:T(128)}, bf16[2,512,384]{2,1,0:T(8,128)(2,1)}, ...), condition=%wide.region_15.16_spmd, body=%wide.region_13.15_spmd.sunk | while | flops 2061629440 | bytes 213811536 | solution.py:263
  361.9 4.7 fusion.129
  368.2 11.4 %multiply_reduce_fusion.3 = (f32[6,512]{1,0:T(8,128)S(1)}, f32[6,512,1024]{2,1,0:T(8,128)}) fusion(f32[6,512,1024]{2,1,0:T(8,128)} %copy-done, f32[6,512]{1,0:T(8,128)S(1)} %dynamic-slice_bitcast_fusion.2, pred[1024]{0:T(1024)(128)(4,1)} %copy-done.21, bf16[512,6,64]{0,2,1:T(8,128)(2,1)S(1)} %bitcast.177, bf16[1024,6,64]{0,2,1:T(8,128)(2,1)S(1)} %bitcast.172), kind=kOutput, calls=%fused_computation.19.clone.1 | convolution fusion | flops 418378752 | bytes 26371072 | tf_op jit(solution)/shard_map/while/body/eval_jaxpr/qhe,khe->hqk/dot_general | solution.py:75
  379.6 6.6 multiply_convert_fusion.4
  399.5 4.7 fusion.129
  405.8 11.4 %multiply_reduce_fusion.3 = (f32[6,512]{1,0:T(8,128)S(1)}, f32[6,512,1024]{2,1,0:T(8,128)}) fusion(f32[6,512,1024]{2,1,0:T(8,128)} %copy-done, f32[6,512]{1,0:T(8,128)S(1)} %dynamic-slice_bitcast_fusion.2, pred[1024]{0:T(1024)(128)(4,1)} %copy-done.21, bf16[512,6,64]{0,2,1:T(8,128)(2,1)S(1)} %bitcast.177, bf16[1024,6,64]{0,2,1:T(8,128)(2,1)S(1)} %bitcast.172), kind=kOutput, calls=%fused_computation.19.clone.1 | convolution fusion | flops 418378752 | bytes 26371072 | tf_op jit(solution)/shard_map/while/body/eval_jaxpr/qhe,khe->hqk/dot_general | solution.py:75
  417.2 6.6 multiply_convert_fusion.4
  432.1 3.2 convolution_bitcast_fusion.3
  435.3 7.1 fusion.60
  442.6 14.7 %reduce-scatter.15.cloned.1.call-done = bf16[2,512,384]{2,1,0:T(8,128)(2,1)} async-done(((bf16[2,1024,384]{2,1,0:T(8,128)(2,1)}), bf16[2,512,384]{2,1,0:T(8,128)(2,1)}) %reduce-scatter.15.cloned.1.call-update) | async-done | bytes 786448 | tf_op jit(solution)/shard_map/reduce_scatter | solution.py:270
  459.5 26.7 %reduce-scatter.13.cloned.1.call-done = bf16[2,512,384]{2,1,0:T(8,128)(2,1)} async-done(((bf16[2,1024,384]{2,1,0:T(8,128)(2,1)}), bf16[2,512,384]{2,1,0:T(8,128)(2,1)}) %reduce-scatter.13.cloned.1.call-update) | async-done | bytes 786448 | tf_op jit(solution)/shard_map/reduce_scatter | solution.py:267
  486.3 4.8 bitcast_convert_fusion
  493.0 7.0 convolution_bitcast_fusion.1
  500.6 7.3 convolution_bitcast_fusion
  508.6 5.9 convolution_bitcast_fusion.2
  515.8 36.8 %reduce-scatter.27.cloned.1.call-done = f32[192,1]{1,0:T(8,128)} async-done(((f32[1536,1]{1,0:T(8,128)}), f32[192,1]{1,0:T(8,128)}) %reduce-scatter.27.cloned.1.call-update) | async-done | bytes 784
  553.6 66.3 %reduce-scatter.19.cloned.1.call-done = f32[96,384]{1,0:T(8,128)} async-done(((f32[768,384]{1,0:T(8,128)}), f32[96,384]{1,0:T(8,128)}) %reduce-scatter.19.cloned.1.call-update) | async-done | bytes 147472 | tf_op jit(solution)/shard_map/reduce_scatter | solution.py:322
  621.4 63.2 %reduce-scatter.25.cloned.1.call-done = f32[48,2]{1,0:T(8,128)} async-done(((f32[384,2]{1,0:T(8,128)}), f32[48,2]{1,0:T(8,128)}) %reduce-scatter.25.cloned.1.call-update) | async-done | bytes 400
  685.4 24.5 %all-reduce.27.cloned.1.call-done = (bf16[2,512,768]{2,1,0:T(8,128)(2,1)}, bf16[2,512,768]{2,1,0:T(8,128)(2,1)}) async-done(((bf16[2,512,768]{2,1,0:T(8,128)(2,1)}, bf16[2,512,768]{2,1,0:T(8,128)(2,1)}), (bf16[2,512,768]{2,1,0:T(8,128)(2,1)}, bf16[2,512,768]{2,1,0:T(8,128)(2,1)})) %all-reduce.27.cloned.1.call-update) | async-done | bytes 3145744 | tf_op jit(solution)/shard_map/psum | solution.py:36
  710.0 2.8 fusion.46
  712.8 38.8 %all-reduce.13 = (bf16[768]{0:T(1024)(128)(2,1)S(1)}, bf16[768]{0:T(1024)(128)(2,1)S(1)}, bf16[768]{0:T(1024)(128)(2,1)S(1)}, bf16[768]{0:T(1024)(128)(2,1)S(1)}...) all-reduce(f32[768]{0:T(1024)S(1)} %get-tuple-element.153, ...), channel_id=5, replica_groups=mesh['dp'=8,'ctx'=2,'tp'=2] {'dp'}, use_global_device_ids=true, to_apply=%region_22.23.clone | all-reduce | flops 4608 | bytes 27648
  752.0 5.0 all-reduce.16
  761.2 49.7 %reduce-scatter.21.cloned.1.call-done = f32[96,1536]{1,0:T(8,128)} async-done(((f32[768,1536]{1,0:T(8,128)}), f32[96,1536]{1,0:T(8,128)}) %reduce-scatter.21.cloned.1.call-update) | async-done | bytes 589840 | tf_op jit(solution)/shard_map/reduce_scatter | solution.py:326
  812.7 97.0 %reduce-scatter.23.cloned.1.call-done = f32[96,1536]{1,0:T(8,128)} async-done(((f32[768,1536]{1,0:T(8,128)}), f32[96,1536]{1,0:T(8,128)}) %reduce-scatter.23.cloned.1.call-update) | async-done | bytes 589840 | tf_op jit(solution)/shard_map/reduce_scatter | solution.py:328
  911.5 80.8 %reduce-scatter.17.cloned.1.call-done = f32[96,3,384]{2,0,1:T(8,128)} async-done(((f32[768,3,384]{2,0,1:T(8,128)}), f32[96,3,384]{2,0,1:T(8,128)}) %reduce-scatter.17.cloned.1.call-update) | async-done | bytes 442384 | tf_op jit(solution)/shard_map/reduce_scatter | solution.py:320
  994.0 4.9 fusion.38
  998.9 33.0 %all-reduce.29.cloned.1.call-done = (bf16[96,3,384]{2,0,1:T(8,128)(2,1)}, bf16[96,384]{1,0:T(8,128)(2,1)}, bf16[96,1536]{1,0:T(8,128)(2,1)}, bf16[96,1536]{1,0:T(8,128)(2,1)}) async-done(((bf16[96,3,384]{2,0,1:T(8,128)(2,1)}, bf16[96,384]{1,0:T(8,128)(2,1)}, bf16[96,1536]{1,0:T(8,128)(2,1)}, bf16[96,1536]{1,0:T(8,128)(2,1)}), (bf16[96,3,384]{2,0,1:T(8,128)(2,1)}, bf16[96,384]{1,0:T(8,128)(2,1)}, ...) | async-done | bytes 884752 | tf_op jit(solution)/shard_map/psum | solution.py:334
  (280 shorter events, 100.5 us)
Async XLA Ops:
  7.2 84.3 %copy-start.2 = (bf16[2,512,768]{2,1,0:T(8,128)(2,1)S(1)}, bf16[2,512,768]{2,1,0:T(8,128)(2,1)}, u32[]{:S(2)}) copy-start(bf16[2,512,768]{2,1,0:T(8,128)(2,1)} %param.19) | copy-start | bytes 4718596
  7.2 84.9 %all-gather.7.cloned.1.call-start = ((), (), s32[]{:S(2)}) async-start(), calls=%async_computation.8 | async-start | bytes 1990656 | tf_op jit(solution)/shard_map/all_gather | solution.py:134
  7.9 127.7 %all-gather.9.cloned.1.call-start = ((), (), s32[]{:S(2)}) async-start(), calls=%async_computation.9 | async-start | bytes 2359296 | tf_op jit(solution)/shard_map/all_gather | solution.py:175
  57.3 34.8 %copy-start.28 = (f32[768]{0:T(1024)}, f32[768]{0:T(1024)S(1)}, u32[]{:S(2)}) copy-start(f32[768]{0:T(1024)S(1)} %convert_element_type.232) | copy-start | bytes 9220
  57.3 34.8 %copy-start.41 = (f32[768]{0:T(1024)}, f32[768]{0:T(1024)S(1)}, u32[]{:S(2)}) copy-start(f32[768]{0:T(1024)S(1)} %convert_element_type.234) | copy-start | bytes 9220
  96.6 5.8 copy-start.23
  99.7 54.0 %all-gather.15.cloned.1.call-start = ((), (), s32[]{:S(2)}) async-start(), calls=%async_computation.20 | async-start | bytes 2359296 | tf_op jit(solution)/shard_map/all_gather | solution.py:174
  102.2 102.0 %all-reduce.23.cloned.1.call-start = ((), (), s32[]{:S(2)}) async-start(), calls=%async_computation.10 | async-start | bytes 3145728 | tf_op jit(solution)/shard_map/psum | solution.py:36
  183.7 75.6 %all-gather.11.cloned.1.call-start = ((), (), s32[]{:S(2)}) async-start(), calls=%async_computation.11 | async-start | bytes 2654208 | tf_op jit(solution)/shard_map/all_gather | solution.py:148
  184.3 127.4 %all-gather.13.cloned.1.call-start = ((), (), s32[]{:S(2)}) async-start(), calls=%async_computation.12 | async-start | bytes 2654208 | tf_op jit(solution)/shard_map/all_gather | solution.py:152
  184.8 159.2 %all-reduce.25.cloned.1.call-start = ((), (), s32[]{:S(2)}) async-start(), calls=%async_computation.13 | async-start | bytes 3145728 | tf_op jit(solution)/shard_map/psum | solution.py:36
  185.2 74.1 %copy-start.43 = (f32[768]{0:T(1024)}, f32[768]{0:T(1024)S(1)}, u32[]{:S(2)}) copy-start(f32[768]{0:T(1024)S(1)} %convert_element_type.248) | copy-start | bytes 9220
  185.2 162.9 %copy-start.17 = (f32[768]{0:T(1024)}, f32[768]{0:T(1024)S(1)}, u32[]{:S(2)}) copy-start(f32[768]{0:T(1024)S(1)} %convert_element_type.244) | copy-start | bytes 9220
  185.2 162.9 %copy-start.32 = (f32[768]{0:T(1024)}, f32[768]{0:T(1024)S(1)}, u32[]{:S(2)}) copy-start(f32[768]{0:T(1024)S(1)} %convert_element_type.246) | copy-start | bytes 9220
  186.0 162.2 %copy-start.19 = (pred[2,512]{1,0:T(4,128)(4,1)}, pred[2,512]{1,0:T(4,128)(4,1)S(1)}, u32[]{:S(2)}) copy-start(pred[2,512]{1,0:T(4,128)(4,1)S(1)} %broadcast_compare_fusion) | copy-start | bytes 3076
  206.3 141.8 %copy-start.26 = (f32[2,512]{1,0:T(2,128)}, f32[2,512]{1,0:T(2,128)S(1)}, u32[]{:S(2)}) copy-start(f32[2,512]{1,0:T(2,128)S(1)} %broadcast_multiply_fusion.4) | copy-start | bytes 12292
  207.2 140.9 %copy-start.34 = (f32[2,512]{1,0:T(2,128)}, f32[2,512]{1,0:T(2,128)S(1)}, u32[]{:S(2)}) copy-start(f32[2,512]{1,0:T(2,128)S(1)} %add_rsqrt_fusion) | copy-start | bytes 12292
  311.7 9.6 copy-start.46
  325.0 132.3 %reduce-scatter.15.cloned.1.call-start = ((), (), s32[]{:S(2)}) async-start(), calls=%async_computation.15 | async-start | bytes 2359296 | tf_op jit(solution)/shard_map/reduce_scatter | solution.py:270
  344.1 4.1 copy-start.9
  344.1 4.1 copy-start.10
  356.4 5.5 copy-start.21
  361.9 4.7 copy-start
  368.1 11.5 %copy-start.1 = (f32[6,512,1024]{2,1,0:T(8,128)S(1)}, f32[6,512,1024]{2,1,0:T(8,128)}, u32[]{:S(2)}) copy-start(f32[6,512,1024]{2,1,0:T(8,128)} %copy-done) | copy-start | bytes 37748740 | tf_op jit(solution)/shard_map/while
  368.1 11.5 %copy-start.22 = (pred[1024]{0:T(1024)(128)(4,1)S(1)}, pred[1024]{0:T(1024)(128)(4,1)}, u32[]{:S(2)}) copy-start(pred[1024]{0:T(1024)(128)(4,1)} %copy-done.21) | copy-start | bytes 3076 | tf_op jit(solution)/shard_map/while
  394.0 5.5 copy-start.21
  399.5 4.7 copy-start
  405.8 11.5 %copy-start.1 = (f32[6,512,1024]{2,1,0:T(8,128)S(1)}, f32[6,512,1024]{2,1,0:T(8,128)}, u32[]{:S(2)}) copy-start(f32[6,512,1024]{2,1,0:T(8,128)} %copy-done) | copy-start | bytes 37748740 | tf_op jit(solution)/shard_map/while
  405.8 11.5 %copy-start.22 = (pred[1024]{0:T(1024)(128)(4,1)S(1)}, pred[1024]{0:T(1024)(128)(4,1)}, u32[]{:S(2)}) copy-start(pred[1024]{0:T(1024)(128)(4,1)} %copy-done.21) | copy-start | bytes 3076 | tf_op jit(solution)/shard_map/while
  429.8 56.5 %reduce-scatter.13.cloned.1.call-start = ((), (), s32[]{:S(2)}) async-start(), calls=%async_computation.14 | async-start | bytes 2359296 | tf_op jit(solution)/shard_map/reduce_scatter | solution.py:267
  430.5 122.1 %reduce-scatter.27.cloned.1.call-start = ((), (), s32[]{:S(2)}) async-start(), calls=%async_computation.22 | async-start | bytes 884736
  431.8 188.1 %reduce-scatter.19.cloned.1.call-start = ((), (), s32[]{:S(2)}) async-start(), calls=%async_computation.17 | async-start | bytes 1327104 | tf_op jit(solution)/shard_map/reduce_scatter | solution.py:322
  435.2 249.4 %reduce-scatter.25.cloned.1.call-start = ((), (), s32[]{:S(2)}) async-start(), calls=%async_computation.21 | async-start | bytes 221184
  435.3 7.1 copy-start.14
  435.3 51.0 %copy-start.47 = (bf16[768,3,384]{2,0,1:T(8,128)(2,1)S(1)}, bf16[768,3,384]{2,0,1:T(8,128)(2,1)}, u32[]{:S(2)}) copy-start(bf16[768,3,384]{2,0,1:T(8,128)(2,1)} %all-gather.7.cloned.1.call-done) | copy-start | bytes 5308420
  459.5 250.5 %all-reduce.27.cloned.1.call-start = ((), (), s32[]{:S(2)}) async-start(), calls=%async_computation.23 | async-start | bytes 6291456 | tf_op jit(solution)/shard_map/psum | solution.py:36
  486.3 4.9 copy-start.27
  486.3 4.9 copy-start.33
  486.3 4.9 copy-start.35
  486.3 4.9 copy-start.44
  491.1 319.7 %reduce-scatter.21.cloned.1.call-start = ((), (), s32[]{:S(2)}) async-start(), calls=%async_computation.18 | async-start | bytes 5308416 | tf_op jit(solution)/shard_map/reduce_scatter | solution.py:326
  500.0 409.7 %reduce-scatter.23.cloned.1.call-start = ((), (), s32[]{:S(2)}) async-start(), calls=%async_computation.19 | async-start | bytes 5308416 | tf_op jit(solution)/shard_map/reduce_scatter | solution.py:328
  508.0 484.3 %reduce-scatter.17.cloned.1.call-start = ((), (), s32[]{:S(2)}) async-start(), calls=%async_computation.16 | async-start | bytes 3981312 | tf_op jit(solution)/shard_map/reduce_scatter | solution.py:320
  514.5 198.3 %copy-start.36 = (f32[768]{0:T(1024)S(1)}, f32[768]{0:T(1024)}, u32[]{:S(2)}) copy-start(f32[768]{0:T(1024)} %get-tuple-element.151) | copy-start | bytes 9220
  514.5 198.3 %copy-start.37 = (f32[768]{0:T(1024)S(1)}, f32[768]{0:T(1024)}, u32[]{:S(2)}) copy-start(f32[768]{0:T(1024)} %get-tuple-element.157) | copy-start | bytes 9220
  514.5 198.3 %copy-start.38 = (f32[768]{0:T(1024)S(1)}, f32[768]{0:T(1024)}, u32[]{:S(2)}) copy-start(f32[768]{0:T(1024)} %get-tuple-element.222) | copy-start | bytes 9220
  514.5 198.3 %copy-start.39 = (f32[768]{0:T(1024)S(1)}, f32[768]{0:T(1024)}, u32[]{:S(2)}) copy-start(f32[768]{0:T(1024)} %get-tuple-element.232) | copy-start | bytes 9220
  514.6 517.4 %all-reduce.29.cloned.1.call-start = ((), (), s32[]{:S(2)}) async-start(), calls=%async_computation.24 | async-start | bytes 1769472 | tf_op jit(solution)/shard_map/psum | solution.py:334
  (26 other events, 44.0 us)
Sparse Core Ops, SparseCore 0:
  10.2 49.5 all-gather.6
  99.9 24.4 all-gather.8
  126.5 27.1 all-gather.14
  183.8 20.3 all-reduce.22
  206.2 52.9 all-gather.10
  261.3 50.3 all-gather.12
  325.1 18.8 all-reduce.24
  429.9 27.3 reduce-scatter.14
  460.1 26.1 reduce-scatter.12
  489.4 63.1 reduce-scatter.26
  556.1 63.7 reduce-scatter.18
  623.6 60.9 reduce-scatter.24
  687.6 22.3 all-reduce.26
  713.5 97.3 reduce-scatter.20
  814.3 95.2 reduce-scatter.22
  913.2 79.0 reduce-scatter.16
  995.7 36.1 all-reduce.28
where the time goes:
time: 1050 us
  waiting for transfers between devices  645 us (61%)
  blocking collectives  146 us (14%)
  matrix products  120 us (11%)
  other arithmetic  68.5 us (7%)
  local copies, waits for them, and re-layouts  47.6 us (5%)
  between operations  16.7 us (2%)
    unnamed x19, waiting for transfers between devices  103 us
    reduce_scatter x1, waiting for transfers between devices, on_device(): lax.psum_scatter(grad_list[10], 'dp', scatter_dimension=0, tiled=True)  97 us
    reduce_scatter x1, waiting for transfers between devices, on_device(): lax.psum_scatter(grad_list[2], 'dp', scatter_dimension=0, tiled=True)  80.8 us
    unnamed x2, blocking collectives  78.7 us
    reduce_scatter x1, waiting for transfers between devices, on_device(): lax.psum_scatter(grad_list[4], 'dp', scatter_dimension=0, tiled=True)  66.3 us
    psum x3, waiting for transfers between devices, tensor_sum(): return lax.psum(partial_sum.astype(jnp.bfloat16), 'tp').astype(jnp.float32)  61.3 us
    all_gather x1, waiting for transfers between devices, on_device(): lax.all_gather(w_fc, 'dp', axis=0, tiled=True)  52 us
    reduce_scatter x1, waiting for transfers between devices, on_device(): lax.psum_scatter(grad_list[8], 'dp', scatter_dimension=0, tiled=True)  49.7 us
  transfers between devices with their start and end apart: 17, of which 15 were waited for; matrix products, arithmetic and copies ran while one was open for 8% of the time, Pallas kernels for 0%

commit v1 on v0

v1 whole, which is shorter than its diff:
```python
import functools

import jax
import jax.numpy as jnp
from jax import lax
from jax.experimental import pallas as pl
from jax.experimental.pallas import tpu as pltpu
from jax.sharding import PartitionSpec as P

HD = 64
EPS = 1e-05
NEG = -1e30
GELU = 1.702
SCALE = HD ** (-0.5)
F32 = jnp.float32
BF16 = jnp.bfloat16
MESH = pl.DeviceIdType.MESH
LIMIT = 60 * 2**20
NN = (((1,), (0,)), ((), ()))
NT = (((1,), (1,)), ((), ()))


def dot(a, b, dims=NN):
    return lax.dot_general(a, b, dims, preferred_element_type=F32)


class Net:
    def __init__(self, send, recv):
        self.send, self.recv, self.used, self.all = send, recv, 0, []

    def put(self, src, dst, dev):
        k = self.used
        self.used += 1
        copy = pltpu.make_async_remote_copy(
            src_ref=src, dst_ref=dst, send_sem=self.send.at[k], recv_sem=self.recv.at[k],
            device_id=dev, device_id_type=MESH,
        )
        copy.start()
        self.all.append(copy)
        return copy

    def finish(self):
        for copy in self.all:
            copy.wait_send()


class Place:
    def __init__(self, n_dp):
        self.d = lax.axis_index("dp")
        self.c = lax.axis_index("ctx")
        self.t = lax.axis_index("tp")
        self.n_o = n_dp // 2
        self.o, self.i = self.d // 2, self.d % 2

    def outer(self, s):
        return (lax.rem(self.o + s, self.n_o) * 2 + self.i, self.c, self.t)

    def from_outer(self, s):
        return lax.rem(self.o + self.n_o - s, self.n_o) * 2 + self.i

    @property
    def inner(self):
        return (self.o * 2 + 1 - self.i, self.c, self.t)

    @property
    def ctx(self):
        return (self.d, 1 - self.c, self.t)

    @property
    def tp(self):
        return (self.d, self.c, 1 - self.t)

    def barrier(self):
        sem = pltpu.get_barrier_semaphore()
        peers = [self.outer(s) for s in range(1, self.n_o)] + [self.inner, self.ctx, self.tp]
        for peer in peers:
            pl.semaphore_signal(sem, 1, device_id=peer, device_id_type=MESH)
        pl.semaphore_wait(sem, len(peers))


def gather_kernel(
    n_dp, tok, cot, small, wq, wo, wf, wp,
    xs, gs, small_all, wq_all, wo_all, wf_all, wp_all, send, recv, local,
):
    me = Place(n_dp)
    net = Net(send, recv)
    d, c, t = me.d, me.c, me.t
    shifts = list(range(1, me.n_o))
    half = tok.shape[1]
    quarter = half // 2
    rows = wf.shape[0]
    hrow = rows // 2
    me.barrier()

    def own(src, dst, k):
        copy = pltpu.make_async_copy(src, dst, local.at[k])
        copy.start()
        return copy

    def whole(src, dst):
        return [net.put(src, dst.at[d], me.outer(s)) for s in shifts] + [
            net.put(src, dst.at[d], me.inner)
        ]

    def cut(ref, dev):
        return ref.at[dev, pl.ds(c * hrow, hrow)]

    def spread(src, dst):
        return [
            net.put(src.at[pl.ds(c * hrow, hrow)], cut(dst, d), me.outer(s)) for s in shifts
        ]

    mine = pl.ds(c * half + t * quarter, quarter)
    theirs = pl.ds((1 - c) * half + t * quarter, quarter)
    tok_y = net.put(tok.at[1 - c, pl.ds(t * quarter, quarter)], xs.at[mine], me.ctx)
    small_o = whole(small, small_all)
    q_o = whole(wq, wq_all)
    o_o = whole(wo, wo_all)
    cot_y = net.put(cot.at[1 - c, pl.ds(t * quarter, quarter)], gs.at[mine], me.ctx)
    f_o = spread(wf, wf_all)
    p_o = spread(wp, wp_all)
    locals_ = [
        own(tok.at[c], xs.at[pl.ds(c * half, half)], 0),
        own(cot.at[c], gs.at[pl.ds(c * half, half)], 1),
        own(small, small_all.at[d], 2),
        own(wq, wq_all.at[d], 3),
        own(wo, wo_all.at[d], 4),
        own(wf, wf_all.at[d], 5),
        own(wp, wp_all.at[d], 6),
    ]

    def relay(copies, dst):
        out = []
        for s, copy in zip(shifts, copies):
            copy.wait_recv()
            src = dst.at[me.from_outer(s)]
            out.append(net.put(src, src, me.inner))
        return out

    rest = relay(small_o, small_all)
    tok_y.wait_recv()
    rest.append(net.put(xs.at[theirs], xs.at[theirs], me.tp))
    rest += relay(q_o, wq_all)
    rest += relay(o_o, wo_all)
    cot_y.wait_recv()
    rest.append(net.put(gs.at[theirs], gs.at[theirs], me.tp))
    rest += [small_o[-1], q_o[-1], o_o[-1]]

    def wide(copies, src, dst):
        out, over = [], [net.put(src.at[pl.ds(c * hrow, hrow)], cut(dst, d), me.inner)]
        for s, copy in zip(shifts, copies):
            copy.wait_recv()
            piece = cut(dst, me.from_outer(s))
            over.append(net.put(piece, piece, me.inner))
            out.append(net.put(piece, piece, me.ctx))
        for s, copy in zip([0] + shifts, over):
            copy.wait_recv()
            piece = cut(dst, lax.rem(me.o + me.n_o - s, me.n_o) * 2 + 1 - me.i)
            out.append(net.put(piece, piece, me.ctx))
        return out

    rest += wide(f_o, wf, wf_all)
    rest += wide(p_o, wp, wp_all)
    for copy in rest:
        copy.wait_recv()
    net.finish()
    for copy in locals_:
        copy.wait()


def add_rows(dst, parts, rows, step):
    @pl.loop(0, rows // step)
    def _(j):
        at = pl.ds(pl.multiple_of(j * step, step), step)
        total = parts[0][at, :].astype(F32)
        for part in parts[1:]:
            total = total + part[at, :].astype(F32)
        dst[at, :] = total.astype(dst.dtype)


def reduce_kernel(
    n_dp, gq, go, gf, gp, small, out_seq, tok_seq,
    rq, ro, rf, rp, rsmall, out, gtok,
    xq, zq, sq, yq, xo, zo, so, yo, xf, zf, sf, yf, xp, zp, sp, yp, xm, zm, sm, ym,
    send, recv, local,
):
    me = Place(n_dp)
    net = Net(send, recv)
    d, c, t = me.d, me.c, me.t
    shifts = list(range(1, me.n_o))
    half = out.shape[1]
    quarter = half // 2
    me.barrier()

    mine = pl.ds((1 - c) * half + t * quarter, quarter)
    final = []
    seq_y = []
    for src, dst in ((out_seq, out), (tok_seq, gtok)):
        seq_y.append(net.put(src.at[mine], dst.at[c, pl.ds(t * quarter, quarter)], me.ctx))
    locals_ = []
    for k, (src, dst) in enumerate(((out_seq, out), (tok_seq, gtok))):
        copy = pltpu.make_async_copy(src.at[pl.ds(c * half, half)], dst.at[c], local.at[k])
        copy.start()
        locals_.append(copy)

    def outer_of(s):
        return lax.rem(me.o + s, me.n_o)

    def first(g, x):
        return [
            net.put(g.at[outer_of(s) * 2 + 1 - me.i], x.at[s], me.inner)
            for s in shifts + [0]
        ]

    def second(g, x, z, sums, copies, rows, step):
        out = []
        for s, copy in zip(shifts + [0], copies):
            copy.wait_recv()
            add_rows(sums.at[s], [g.at[outer_of(s) * 2 + me.i], x.at[s]], rows, step)
            if s:
                out.append(net.put(sums.at[s], z.at[s - 1], me.outer(s)))
        return out

    def third(z, sums, y, copies, rows, step):
        for copy in copies:
            copy.wait_recv()
        add_rows(y.at[0], [sums.at[0]] + [z.at[s - 1] for s in shifts], rows, step)
        return net.put(y.at[0], y.at[1], me.ctx)

    def fourth(y, r, copy, rows, step):
        copy.wait_recv()
        add_rows(r, [y.at[0], y.at[1]], rows, step)

    groups = [
        (gp, xp, zp, sp, yp, rp, 16),
        (gf, xf, zf, sf, yf, rf, 16),
        (go, xo, zo, so, yo, ro, 16),
        (gq, xq, zq, sq, yq, rq, 16),
        (small, xm, zm, sm, ym, rsmall, 8),
    ]
    ones = [first(g, x) for g, x, _, _, _, _, _ in groups]
    twos = []
    for copy, (src, dst) in zip(seq_y, ((out_seq, out), (tok_seq, gtok))):
        copy.wait_recv()
        place = dst.at[1 - c, pl.ds(t * quarter, quarter)]
        final.append(net.put(place, place, me.tp))
    for (g, x, z, s, y, r, step), copies in zip(groups, ones):
        twos.append(second(g, x, z, s, copies, r.shape[0], step))
    threes = []
    for (g, x, z, s, y, r, step), copies in zip(groups, twos):
        threes.append(third(z, s, y, copies, r.shape[0], step))
    for (g, x, z, s, y, r, step), copy in zip(groups, threes):
        fourth(y, r, copy, r.shape[0], step)
    for copy in final:
        copy.wait_recv()
    net.finish()
    for copy in locals_:
        copy.wait()


def norm(x):
    centred = x - jnp.mean(x, axis=-1, keepdims=True)
    inv = lax.rsqrt(jnp.mean(centred * centred, axis=-1, keepdims=True) + EPS)
    return centred * inv, inv


def block(j, size):
    return pl.ds(pl.multiple_of(j * size, size), size)


def forward_kernel(
    length, xs, vec, bq, bv, wq, wo, q, k, v, kt, h1t, o, ot, pt, part, vt
):
    rows, width = xs.shape
    cols = q.shape[1]
    step = 256

    @pl.loop(0, rows // step)
    def _(j):
        at = block(j, step)
        n, _ = norm(xs[at, :].astype(F32))
        h1 = (n * vec[0:1, :] + vec[1:2, :]).astype(BF16)
        h1t[:, at] = h1.T
        proj = dot(h1, wq[...])
        q[at, :] = (proj[:, :cols] + bq[...]).astype(BF16) * SCALE
        kk = proj[:, cols : 2 * cols].astype(BF16)
        vv = (proj[:, 2 * cols :] + bv[...]).astype(BF16)
        k[at, :] = kk
        v[at, :] = vv
        kt[:, at] = kk.T
        vt[:, at] = vv.T

    live = lax.broadcasted_iota(jnp.int32, (rows, step), 0) < length[0]
    side = lax.broadcasted_iota(jnp.int32, (step, 128), 1) // HD

    @pl.loop(0, cols // 128)
    def _(p):
        pair = block(p, 128)

        @pl.loop(0, rows // step)
        def _(j):
            at = block(j, step)
            for hh in range(2):
                qm = jnp.where(side == hh, q[at, pair], jnp.zeros((), BF16))
                s = dot(k[:, pair], qm, NT)
                s = jnp.where(live, s, NEG)
                e = jnp.exp(s - jnp.max(s, axis=0, keepdims=True))
                pb = (e * (1.0 / jnp.sum(e, axis=0, keepdims=True))).astype(BF16)
                pt[p * 2 + hh, :, at] = pb
                head = block(p * 2 + hh, HD)
                ot[head, at] = dot(vt[head, :], pb).astype(BF16)

    @pl.loop(0, rows // step)
    def _(j):
        at = block(j, step)
        ob = ot[:, at].T
        o[at, :] = ob
        part[at, :] = dot(ob, wo[...], NT).astype(BF16)


def mlp_kernel(
    length, xs, gs, vec, bf, p0, p1, wf, wp, r1, a, du, h2t, gt, part2, part3
):
    rows, width = xs.shape
    step = 256

    @pl.loop(0, rows // step)
    def _(j):
        at = block(j, step)
        mid = xs[at, :].astype(F32) + (p0[at, :].astype(F32) + p1[at, :].astype(F32)) + vec[2:3, :]
        r1[at, :] = mid
        n, _ = norm(mid)
        h2 = (n * vec[3:4, :] + vec[4:5, :]).astype(BF16)
        h2t[:, at] = h2.T
        live = j * step + lax.broadcasted_iota(jnp.int32, (step, width), 0) < length[0]
        g = jnp.where(live, gs[at, :], jnp.zeros((), BF16))
        gt[:, at] = g.T
        u = dot(h2, wf[...]) + bf[...]
        s = jax.nn.sigmoid(GELU * u)
        act = (u * s).astype(BF16)
        a[at, :] = act
        part2[at, :] = dot(act, wp[...], NT).astype(BF16)
        slope = s * (1.0 + GELU * u * (1.0 - s))
        dub = (dot(g, wp[...]) * slope).astype(BF16)
        du[at, :] = dub
        part3[at, :] = dot(dub, wf[...], NT).astype(BF16)


def weights_kernel(gt, h2t, a, du, gp, gf, bp, bfg):
    width = gt.shape[0]
    step = 128

    @pl.loop(0, width // step)
    def _(j):
        at = block(j, step)
        gp[at, :] = dot(gt[at, :], a[...]).astype(BF16)
        gf[at, :] = dot(h2t[at, :], du[...]).astype(BF16)

    bp[...] = jnp.zeros_like(bp)
    bfg[...] = jnp.zeros_like(bfg)

    @pl.loop(0, du.shape[0] // 128)
    def _(j):
        at = block(j, 128)
        bfg[...] += jnp.sum(du[at, :].astype(F32), axis=0, keepdims=True)
        bp[...] += jnp.sum(gt[:, at].astype(F32).T, axis=0, keepdims=True)


def middle_kernel(
    length, gs, vec, r1, p2a, p2b, p3a, p3b, o, wo, out, dr1, do, go, sums, dt
):
    rows, width = gs.shape
    step = 256
    sums[...] = jnp.zeros_like(sums)

    @pl.loop(0, rows // step)
    def _(j):
        at = block(j, step)
        mid = r1[at, :]
        out[at, :] = (
            mid + (p2a[at, :].astype(F32) + p2b[at, :].astype(F32)) + vec[5:6, :]
        ).astype(BF16)
        n, inv = norm(mid)
        dh = p3a[at, :].astype(F32) + p3b[at, :].astype(F32)
        e = dh * vec[3:4, :]
        live = j * step + lax.broadcasted_iota(jnp.int32, (step, width), 0) < length[0]
        g = jnp.where(live, gs[at, :].astype(F32), 0.0)
        grad = g + inv * (
            e - jnp.mean(e, axis=-1, keepdims=True) - n * jnp.mean(e * n, axis=-1, keepdims=True)
        )
        dr1[at, :] = grad
        sums[0:1, :] += jnp.sum(grad, axis=0, keepdims=True)
        sums[1:2, :] += jnp.sum(dh * n, axis=0, keepdims=True)
        sums[2:3, :] += jnp.sum(dh, axis=0, keepdims=True)
        gb = grad.astype(BF16)
        dt[:, at] = gb.T
        do[at, :] = dot(gb, wo[...]).astype(BF16)

    @pl.loop(0, width // step)
    def _(j):
        at = block(j, step)
        go[at, :] = dot(dt[at, :], o[...]).astype(BF16)


def backward_kernel(
    q, k, v, kt, h1t, ot, pt, do, wq, gq, part, sums, dot_t, dst, dqt, dqkv
):
    rows, cols = q.shape
    step = 256
    side = lax.broadcasted_iota(jnp.int32, (step, 128), 1) // HD
    side_all = lax.broadcasted_iota(jnp.int32, (rows, 128), 1) // HD
    zero = jnp.zeros((), BF16)

    @pl.loop(0, rows // step)
    def _(j):
        at = block(j, step)
        dot_t[:, at] = do[at, :].T

    @pl.loop(0, cols // 128)
    def _(p):
        pair = block(p, 128)
        for hh in range(2):
            head = block(p * 2 + hh, HD)

            @pl.loop(0, rows // step)
            def _(j):
                at = block(j, step)
                inner = jnp.sum(
                    dot_t[head, at].astype(F32) * ot[head, at].astype(F32), axis=0, keepdims=True
                )
                dp = dot(v[:, pair], jnp.where(side == hh, do[at, pair], zero), NT)
                ds = (pt[p * 2 + hh, :, at].astype(F32) * (dp - inner)).astype(BF16)
                dst[hh, :, at] = ds
                dqt[head, at] = dot(kt[head, :], ds)

        qp = q[:, pair]
        dp_ = do[:, pair]
        dk = dot(dst[0], jnp.where(side_all == 0, qp, zero)) + dot(
            dst[1], jnp.where(side_all == 1, qp, zero)
        )
        dv = dot(pt[p * 2], jnp.where(side_all == 0, dp_, zero)) + dot(
            pt[p * 2 + 1], jnp.where(side_all == 1, dp_, zero)
        )
        dqkv[:, pl.ds(pl.multiple_of(cols + p * 128, 128), 128)] = dk.astype(BF16)
        dqkv[:, pl.ds(pl.multiple_of(2 * cols + p * 128, 128), 128)] = dv.astype(BF16)

    sums[...] = jnp.zeros_like(sums)

    @pl.loop(0, rows // step)
    def _(j):
        at = block(j, step)
        dqkv[at, 0:cols] = (dqt[:, at].T * SCALE).astype(BF16)
        low = dqkv[at, :]
        sums[0:1, :] += jnp.sum(low.astype(F32), axis=0, keepdims=True)
        part[at, :] = dot(low, wq[...], NT).astype(BF16)

    @pl.loop(0, h1t.shape[0] // step)
    def _(j):
        at = block(j, step)
        gq[at, :] = dot(h1t[at, :], dqkv[...]).astype(BF16)


def last_kernel(xs, vec, dr1, pa, pb, gtok, sums):
    rows, width = xs.shape
    step = 256
    sums[...] = jnp.zeros_like(sums)

    @pl.loop(0, rows // step)
    def _(j):
        at = block(j, step)
        n, inv = norm(xs[at, :].astype(F32))
        dh = pa[at, :].astype(F32) + pb[at, :].astype(F32)
        e = dh * vec[0:1, :]
        gtok[at, :] = (
            dr1[at, :]
            + inv
            * (e - jnp.mean(e, axis=-1, keepdims=True) - n * jnp.mean(e * n, axis=-1, keepdims=True))
        ).astype(BF16)
        sums[0:1, :] += jnp.sum(dh * n, axis=0, keepdims=True)
        sums[1:2, :] += jnp.sum(dh, axis=0, keepdims=True)


VM = pl.BlockSpec(memory_space=pltpu.VMEM)
SM = pl.BlockSpec(memory_space=pltpu.SMEM)
ANY = pl.BlockSpec(memory_space=pl.ANY)


def call(body, ins, outs, scratch=(), specs=None, out_specs=None, name=None, cid=None):
    params = dict(vmem_limit_bytes=LIMIT)
    if cid is not None:
        params.update(collective_id=cid, has_side_effects=True)
    return pl.pallas_call(
        body,
        out_shape=[jax.ShapeDtypeStruct(s, t) for s, t in outs],
        in_specs=specs or [VM] * len(ins),
        out_specs=out_specs or [VM] * len(outs),
        scratch_shapes=list(scratch),
        name=name,
        compiler_params=pltpu.CompilerParams(**params),
    )(*ins)


def on_device(n_dp, tokens, lengths, ln1_gain, ln1_bias, w_qkv, qv_bias, w_out, out_bias,
              ln2_gain, ln2_bias, w_fc, fc_bias, w_proj, proj_bias, cotangent):
    _, half, width = tokens.shape
    rows = 2 * half
    shard = w_fc.shape[0]
    cols = w_out.shape[1]
    ff = w_fc.shape[1]
    dma = pltpu.SemaphoreType.DMA
    ctx = lax.axis_index("ctx")
    length = lax.dynamic_slice(lengths, (ctx,), (1,))
    lines = [ln1_gain, ln1_bias, out_bias, ln2_gain, ln2_bias, proj_bias,
             qv_bias[:, :, 0].T.reshape(shard)] + list(fc_bias[:, 0].reshape(2, shard))
    small = jnp.pad(jnp.stack(lines), ((0, 16 - len(lines)), (0, 128 - shard)))
    wq_own = w_qkv.reshape(shard, 3 * cols)
    if n_dp == 8:
        outs = [((rows, width), BF16), ((rows, width), BF16), ((n_dp, 16, 128), F32),
                ((n_dp, shard, 3 * cols), BF16), ((n_dp, shard, cols), BF16),
                ((n_dp, shard, ff), BF16), ((n_dp, shard, ff), BF16)]
        xs, gs, small_all, wq, wo, wf, wp = call(
            functools.partial(gather_kernel, n_dp),
            (tokens, cotangent, small, wq_own, w_out, w_fc, w_proj), outs,
            [dma((64,)), dma((64,)), dma((7,))], [ANY] * 7, [ANY] * 7, "gather", 1)
    else:
        def whole(a):
            return lax.all_gather(a, "ctx", axis=1, tiled=True)

        xs = lax.dynamic_index_in_dim(whole(tokens), ctx, 0, False)
        gs = lax.dynamic_index_in_dim(whole(cotangent), ctx, 0, False)
        small_all, wq, wo, wf, wp = [
            lax.all_gather(a, "dp") for a in (small, wq_own, w_out, w_fc, w_proj)]
    wq, wo, wf, wp = [a.reshape(n_dp * shard, -1) for a in (wq, wo, wf, wp)]
    vec = small_all[:, :6, :shard].transpose(1, 0, 2).reshape(6, width)
    vec = jnp.pad(vec, ((0, 2), (0, 0)))
    qv = small_all[:, 6, :shard].reshape(n_dp, 2, shard // 2).transpose(1, 0, 2).reshape(2, cols)
    bf = small_all[:, 7:9, :shard].reshape(1, ff)

    act = ((rows, width), BF16)
    head = ((rows, cols), BF16)
    head_t = ((cols, rows), BF16)
    q, k, v, kt, h1t, o, ot, pt, part1 = call(
        forward_kernel, (length, xs, vec, qv[0:1], qv[1:2], wq, wo),
        [head, head, head, head_t, ((width, rows), BF16), head, head_t,
         ((cols // HD, rows, rows), BF16), act],
        [pltpu.VMEM((cols, rows), BF16)], [SM] + [VM] * 6, name="forward")

    def other(a):
        return lax.ppermute(a, "tp", [(0, 1), (1, 0)])

    r1, a, du, h2t, gt, part2, part3 = call(
        mlp_kernel, (length, xs, gs, vec, bf, part1, other(part1), wf, wp),
        [((rows, width), F32), ((rows, ff), BF16), ((rows, ff), BF16),
         ((width, rows), BF16), ((width, rows), BF16), act, act],
        specs=[SM] + [VM] * 8, name="mlp")
    gp, gf, bp, bfg = call(
        weights_kernel, (gt, h2t, a, du),
        [((width, ff), BF16), ((width, ff), BF16), ((1, width), F32), ((1, ff), F32)],
        name="weights")
    out_seq, dr1, do, go, sums2 = call(
        middle_kernel,
        (length, gs, vec, r1, part2, other(part2), part3, other(part3), o, wo),
        [act, ((rows, width), F32), head, ((width, cols), BF16), ((8, width), F32)],
        [pltpu.VMEM((width, rows), BF16)], [SM] + [VM] * 9, name="middle")
    gq, part4, sums3 = call(
        backward_kernel, (q, k, v, kt, h1t, ot, pt, do, wq),
        [((width, 3 * cols), BF16), act, ((8, 3 * cols), F32)],
        [pltpu.VMEM((cols, rows), BF16), pltpu.VMEM((2, rows, rows), BF16),
         pltpu.VMEM((cols, rows), F32), pltpu.VMEM((rows, 3 * cols), BF16)], name="backward")
    tok_seq, sums1 = call(
        last_kernel, (xs, vec, dr1, part4, other(part4)),
        [act, ((8, width), F32)], name="last")

    gvec = jnp.concatenate([sums1[0:2], sums2[0:3], bp])
    gvec = gvec.reshape(6, n_dp, shard).transpose(1, 0, 2)
    gqv = jnp.stack([sums3[0, :cols], sums3[0, 2 * cols :]]).reshape(2, n_dp, shard // 2)
    gqv = gqv.transpose(1, 0, 2).reshape(n_dp, 1, shard)
    gsmall = jnp.concatenate([gvec, gqv, bfg.reshape(n_dp, 2, shard)], axis=1)
    gsmall = jnp.pad(gsmall, ((0, 0), (0, 7), (0, 128 - shard)))
    gq, go, gf, gp = [a.reshape(n_dp, shard, -1) for a in (gq, go, gf, gp)]
    if n_dp == 8:
        n_o = n_dp // 2
        scratch = []
        for n, r, kind in ((3 * cols, shard, BF16), (cols, shard, BF16), (ff, shard, BF16),
                           (ff, shard, BF16), (128, 16, F32)):
            scratch += [pltpu.VMEM((n_o, r, n), kind), pltpu.VMEM((n_o - 1, r, n), kind),
                        pltpu.VMEM((n_o, r, n), kind), pltpu.VMEM((2, r, n), kind)]
        rq, ro, rf, rp, rs, out, gtok = call(
            functools.partial(reduce_kernel, n_dp),
            (gq, go, gf, gp, gsmall, out_seq, tok_seq),
            [((shard, 3 * cols), F32), ((shard, cols), F32), ((shard, ff), F32),
             ((shard, ff), F32), ((16, 128), F32), ((2, half, width), BF16),
             ((2, half, width), BF16)],
            scratch + [dma((64,)), dma((64,)), dma((2,))],
            [VM] * 5 + [ANY] * 2, [VM] * 5 + [ANY] * 2, "reduce", 2)
    else:
        def summed(a):
            return lax.psum(lax.psum_scatter(a, "dp", scatter_dimension=0), "ctx")

        rq, ro, rf, rp = [summed(a).astype(F32) for a in (gq, go, gf, gp)]
        rs = summed(gsmall)

        def back(a):
            pieces = lax.all_gather(a, "ctx", axis=0)
            return lax.dynamic_slice(pieces, (0, ctx * half, 0), (2, half, width))

        out, gtok = back(out_seq), back(tok_seq)
    line = [rs[j, :shard] for j in range(7)]
    return (out, gtok, line[0], line[1], rq.reshape(shard, 3, cols),
            line[6].reshape(2, shard // 2).T[:, :, None], ro, line[2], line[3], line[4],
            rf, rs[7:9, :shard].reshape(2 * shard, 1), rp, line[5])


def solution(mesh):
    dp, seq = P("dp"), P("dp", "ctx", None)
    wide, flat = P("dp", None, "tp"), P("dp", "tp")
    params = (dp, dp, wide, wide, flat, dp, dp, dp, flat, flat, flat, dp)
    return jax.shard_map(
        functools.partial(on_device, mesh.shape["dp"]),
        mesh=mesh,
        in_specs=(seq, dp) + params + (seq,),
        out_specs=(seq, seq) + params,
        check_vma=False,
    )
```

time: 1050 us -> 370 us (0.35)
  waiting for transfers between devices: 645 us -> 7.45 us
  Pallas kernels: 0 us -> 331 us
  blocking collectives: 146 us -> 0 us
  matrix products: 120 us -> 0 us
  other arithmetic: 68.5 us -> 1.4 us
  local copies, waits for them, and re-layouts: 47.6 us -> 27.1 us
  between operations: 16.7 us -> 0.74 us
    reduce_scatter x6 -> x0, waiting for transfers between devices: 335 us -> none  [the longest x1 97 us: on_device(): lax.psum_scatter(grad_list[10], 'dp', scatter_dimension=0, tiled=True)]
    pallas_call x0 -> x8, Pallas kernels: none -> 331 us  [call(): pl.pallas_call(body, out_shape=[jax.ShapeDtypeStruct(s, t) for s, t in ou...]
    dot_general x26 -> x0, matrix products: 120 us -> none  [the longest x2 22.9 us: attend_back_one(): jnp.einsum('qhe,khe->hqk', grad_heads, value_heads, preferred_element_typ...]
    all_gather x5 -> x0, waiting for transfers between devices: 113 us -> none  [the longest x1 52 us: on_device(): lax.all_gather(w_fc, 'dp', axis=0, tiled=True)]
    unnamed x19 -> x0, waiting for transfers between devices: 103 us -> none
    psum x4 -> x0, waiting for transfers between devices: 94.3 us -> none  [the longest x3 61.3 us: tensor_sum(): return lax.psum(partial_sum.astype(jnp.bfloat16), 'tp').astype(jnp.float32)]
    unnamed x2 -> x0, blocking collectives: 78.7 us -> none
    all_gather x2 -> x0, blocking collectives: 62.1 us -> none  [the longest x1 31.5 us: on_device(): lax.all_gather(w_out, 'dp', axis=0, tiled=True)]
  transfers between devices with their start and end apart: 17 -> 4, of which waited for: 15 -> 3; matrix products, arithmetic and copies ran while one was open for 8% -> 1% of each run, Pallas kernels for 0% -> 4%
where the time goes in v1:
time: 370 us; the launch traced here: 368 us
  Pallas kernels  331 us (89%)
  local copies, waits for them, and re-layouts  27.1 us (7%)
  waiting for transfers between devices  7.45 us (2%)
    pallas_call x8, Pallas kernels, call(): pl.pallas_call(body, out_shape=[jax.ShapeDtypeStruct(s, t) for s, t in ou...  331 us
    unnamed x27, local copies, waits for them, and re-layouts  9.69 us
    ppermute x4, waiting for transfers between devices, other(): return lax.ppermute(a, 'tp', [(0, 1), (1, 0)])  7.45 us
  transfers between devices with their start and end apart: 4, of which 3 were waited for; matrix products, arithmetic and copies ran while one was open for 1% of the time, Pallas kernels for 4%

profile of v1, /device:TPU:0, one launch (start us, length us, event | category | flops | bytes accessed | tf_op | source)
XLA Modules:
  0.0 368.2 jit_solution(4517252025804987245)
XLA Ops:
  0.6 0.8 stack_reshape.3
  1.4 0.8 slice_bitcast_fusion.7
  2.2 1.6 copy.43
  3.9 0.8 stack.30
  4.6 0.6 pad.12.small
  5.2 92.4 %gather.1 = (bf16[1024,768]{1,0:T(8,128)(2,1)}, bf16[1024,768]{1,0:T(8,128)(2,1)}, f32[8,16,128]{2,1,0:T(8,128)}, bf16[8,96,1152]{2,1,0:T(8,128)(2,1)}, bf16[8,9...) custom-call(bf16[2,512,768]{2,1,0:T(8,128)(2,1)} %tok.1, ...), custom_call_target="tpu_custom_call" | custom-call | tf_op jit(solution)/shard_map/gather/pallas_call | solution.py:492
  97.7 0.8 slice_reduce_fusion
  98.5 0.8 slice_bitcast_fusion
  99.3 0.6 slice.64.bv
  100.0 0.6 slice.62.bq
  100.6 0.1 reshape.85
  100.7 0.6 pad.13.vec
  101.3 0.6 dynamic_slice.3.length
  101.9 38.3 %forward.1 = (bf16[1024,384]{1,0:T(8,128)(2,1)}, bf16[1024,384]{1,0:T(8,128)(2,1)}, bf16[1024,384]{1,0:T(8,128)(2,1)}, bf16[384,1024]{1,0:T(8,128)(2,1)}, bf16[7...) custom-call(s32[1]{0:T(128)} %dynamic_slice.3.length, ...), custom_call_target="tpu_custom_call" | custom-call | tf_op jit(solution)/shard_map/forward/pallas_call | solution.py:492
  140.2 0.8 slice.65
  141.0 0.7 reshape.88.bf
  141.7 2.1 collective-permute-done.p1
  143.8 1.2 copy-done
  145.0 21.7 %mlp.1 = (f32[1024,768]{1,0:T(8,128)}, bf16[1024,1536]{1,0:T(8,128)(2,1)}, bf16[1024,1536]{1,0:T(8,128)(2,1)}, bf16[768,1024]{1,0:T(8,128)(2,1)}, bf16[768,1024]...) custom-call(s32[1]{0:T(128)} %dynamic_slice.3.length, bf16[1024,768]{1,0:T(8,128)(2,1)} %get-tuple-element.58.xs, ...), custom_call_target="tpu_custom_call" | custom-call | tf_op jit(solution)/shard_map/mlp/pallas_call | solution.py:492
  166.6 0.1 collective-permute-start.1
  166.8 0.4 collective-permute-start.2
  167.2 3.1 collective-permute-done.1.p2b
  170.3 2.2 collective-permute-done.2.p3b
  172.5 1.2 copy-done.4
  173.7 13.2 %middle.1 = (bf16[1024,768]{1,0:T(8,128)(2,1)}, f32[1024,768]{1,0:T(8,128)}, bf16[1024,384]{1,0:T(8,128)(2,1)}, bf16[768,384]{1,0:T(8,128)(2,1)}, f32[8,768]{1,0:T(8,128)}) custom-call(s32[1]{0:T(128)} %dynamic_slice.3.length, bf16[1024,768]{1,0:T(8,128)(2,1)} %get-tuple-element.69.gs, f32[8,768]{1,0:T(8,128)} %pad.13.vec, ...), custom_call_target="tpu_custom_call" | custom-call | tf_op jit(solution)/shard_map/middle/pallas_call | solution.py:492
  186.9 34.3 %backward.1 = (bf16[768,1152]{1,0:T(8,128)(2,1)}, bf16[1024,768]{1,0:T(8,128)(2,1)}, f32[8,1152]{1,0:T(8,128)}) custom-call(bf16[1024,384]{1,0:T(8,128)(2,1)} %get-tuple-element.62.q, bf16[1024,384]{1,0:T(8,128)(2,1)} %get-tuple-element.63.k, bf16[1024,384]{1,0:T(8,128)(2,1)} %get-tuple-element.64.v, bf16[384,1024]{1,0:T(8,128)(2,1)} %get-tuple-element.65.kt, ...), custom_call_target="tpu_custom_call" | custom-call | tf_op jit(solution)/shard_map/backward/pallas_call | solution.py:492
  221.2 0.1 collective-permute-start.3
  221.3 13.3 %weights.1 = (bf16[768,1536]{1,0:T(8,128)(2,1)}, bf16[768,1536]{1,0:T(8,128)(2,1)}, f32[1,768]{1,0:T(1,128)}, f32[1,1536]{1,0:T(1,128)}) custom-call(bf16[768,1024]{1,0:T(8,128)(2,1)} %get-tuple-element.80.gt, bf16[768,1024]{1,0:T(8,128)(2,1)} %get-tuple-element.81.h2t, bf16[1024,1536]{1,0:T(8,128)(2,1)} %get-tuple-element.82.a, ...), custom_call_target="tpu_custom_call" | custom-call | tf_op jit(solution)/shard_map/weights/pallas_call | solution.py:492
  234.6 0.7 reduce.2
  235.4 0.7 fusion
  236.1 0.1 reshape.96
  236.2 0.1 reshape.97
  236.3 1.1 copy-done.2
  237.4 7.2 %last.1 = (bf16[1024,768]{1,0:T(8,128)(2,1)}, f32[8,768]{1,0:T(8,128)}) custom-call(bf16[1024,768]{1,0:T(8,128)(2,1)} %get-tuple-element.58.xs, f32[8,768]{1,0:T(8,128)} %pad.13.vec, f32[1024,768]{1,0:T(8,128)} %get-tuple-element.86.dr1, bf16[1024,768]{1,0:T(8,128)(2,1)} %get-tuple-element.87.pa, bf16[1024,768]{1,0:T(8,128)(2,1)} %copy-done.2), custom_call_target="tpu_custom_call" | custom-call | tf_op jit(solution)/shard_map/last/pallas_call | solution.py:492
  244.6 0.7 slice.66
  245.4 0.1 reshape.95
  245.5 0.7 select_maximum_fusion.small
  246.1 110.6 %reduce.10 = (f32[96,1152]{1,0:T(8,128)}, f32[96,384]{1,0:T(8,128)}, f32[96,1536]{1,0:T(8,128)}, f32[96,1536]{1,0:T(8,128)}, f32[16,128]{1,0:T(8,128)}, /*index=...) custom-call(bf16[8,96,1152]{2,1,0:T(8,128)(2,1)} %bitcast.63, bf16[8,96,384]{2,1,0:T(8,128)(2,1)} %bitcast.65, ...), custom_call_target="tpu_custom_call" | custom-call | tf_op jit(solution)/shard_map/reduce/pallas_call | solution.py:492
  356.7 0.7 slice.76
  357.4 1.5 slice_bitcast_fusion.1
  358.9 0.6 reshape.100
  359.5 0.6 reshape_squeeze.8
  360.2 1.8 copy.48
  362.0 2.8 copy.57
  364.8 1.1 copy.58
  365.9 0.7 copy.59
  366.6 0.8 copy.60
  367.4 0.8 copy.61
  (31 shorter events, 0.3 us)
Async XLA Ops:
  5.2 96.1 %copy-start.10 = (s32[2]{0:T(128)S(1)}, s32[2]{0:T(128)}, u32[]{:S(2)}) copy-start(s32[2]{0:T(128)} %param.16) | copy-start | bytes 28
  140.2 3.6 collective-permute-start
  143.8 1.2 copy-start
  166.6 3.6 collective-permute-start.1
  166.8 5.7 %collective-permute-start.2 = (bf16[1024,768]{1,0:T(8,128)(2,1)}, bf16[1024,768]{1,0:T(8,128)(2,1)S(1)}, u32[]{:S(2)}, u32[]{:S(2)}) collective-permute-start(bf16[1024,768]{1,0:T(8,128)(2,1)} %get-tuple-element.75.p3a), channel_id=1, source_target_pairs={{0,1},{1,0},{2,3},{3,2},{4,5},{5,4},{6,7},{7,6},{8,9},{9,8},{10,11... | collective-permute-start | bytes 4718600 | tf_op jit(solution)/shard_map/ppermute | solution.py:549
  170.3 2.3 copy-start.3
  172.5 1.2 copy-start.4
  221.2 15.1 %collective-permute-start.3 = (bf16[1024,768]{1,0:T(8,128)(2,1)}, bf16[1024,768]{1,0:T(8,128)(2,1)S(1)}, u32[]{:S(2)}, u32[]{:S(2)}) collective-permute-start(bf16[1024,768]{1,0:T(8,128)(2,1)} %get-tuple-element.87.pa), channel_id=1, source_target_pairs={{0,1},{1,0},{2,3},{3,2},{4,5},{5,4},{6,7},{7,6},{8,9},{9,8},{10,11... | collective-permute-start | bytes 4718600 | tf_op jit(solution)/shard_map/ppermute | solution.py:549
  221.3 15.0 %copy-start.8 = (f32[8,768]{1,0:T(8,128)S(1)}, f32[8,768]{1,0:T(8,128)}, u32[]{:S(2)}) copy-start(f32[8,768]{1,0:T(8,128)} %get-tuple-element.89) | copy-start | bytes 73732
  236.3 1.1 copy-start.2
  237.4 7.9 %copy-start.9 = (f32[1,768]{1,0:T(1,128)S(1)}, f32[1,768]{1,0:T(1,128)}, u32[]{:S(2)}) copy-start(f32[1,768]{1,0:T(1,128)} %get-tuple-element.90) | copy-start | bytes 9220
  362.0 2.8 copy-start.1
  364.8 1.2 copy-start.7
  364.8 1.8 copy-start.6
  364.8 2.6 copy-start.5

commit v2 on v1

--- a/solution.py
+++ b/solution.py
@@ -28,15 +28,24 @@
     def __init__(self, send, recv):
         self.send, self.recv, self.used, self.all = send, recv, 0, []
 
-    def put(self, src, dst, dev):
-        k = self.used
-        self.used += 1
-        copy = pltpu.make_async_remote_copy(
+    def build(self, k, src, dst, dev):
+        return pltpu.make_async_remote_copy(
             src_ref=src, dst_ref=dst, send_sem=self.send.at[k], recv_sem=self.recv.at[k],
             device_id=dev, device_id_type=MESH,
         )
+
+    def take(self, count):
+        self.used += count
+        return self.used - count
+
+    def make(self, src, dst, dev):
+        copy = self.build(self.take(1), src, dst, dev)
+        self.all.append(copy)
+        return copy
+
+    def put(self, src, dst, dev):
+        copy = self.make(src, dst, dev)
         copy.start()
-        self.all.append(copy)
         return copy
 
     def finish(self):
@@ -45,10 +54,11 @@
 
 
 class Place:
-    def __init__(self, n_dp):
+    def __init__(self, n_dp, direct=True):
         self.d = lax.axis_index("dp")
         self.c = lax.axis_index("ctx")
         self.t = lax.axis_index("tp")
+        self.direct = direct
         self.n_o = n_dp // 2
         self.o, self.i = self.d // 2, self.d % 2
 
@@ -72,100 +82,12 @@
 
     def barrier(self):
         sem = pltpu.get_barrier_semaphore()
-        peers = [self.outer(s) for s in range(1, self.n_o)] + [self.inner, self.ctx, self.tp]
+        peers = [self.tp]
+        if self.direct:
+            peers += [self.outer(s) for s in range(1, self.n_o)] + [self.inner, self.ctx]
         for peer in peers:
             pl.semaphore_signal(sem, 1, device_id=peer, device_id_type=MESH)
         pl.semaphore_wait(sem, len(peers))
-
-
-def gather_kernel(
-    n_dp, tok, cot, small, wq, wo, wf, wp,
-    xs, gs, small_all, wq_all, wo_all, wf_all, wp_all, send, recv, local,
-):
-    me = Place(n_dp)
-    net = Net(send, recv)
-    d, c, t = me.d, me.c, me.t
-    shifts = list(range(1, me.n_o))
-    half = tok.shape[1]
-    quarter = half // 2
-    rows = wf.shape[0]
-    hrow = rows // 2
-    me.barrier()
-
-    def own(src, dst, k):
-        copy = pltpu.make_async_copy(src, dst, local.at[k])
-        copy.start()
-        return copy
-
-    def whole(src, dst):
-        return [net.put(src, dst.at[d], me.outer(s)) for s in shifts] + [
-            net.put(src, dst.at[d], me.inner)
-        ]
-
-    def cut(ref, dev):
-        return ref.at[dev, pl.ds(c * hrow, hrow)]
-
-    def spread(src, dst):
-        return [
-            net.put(src.at[pl.ds(c * hrow, hrow)], cut(dst, d), me.outer(s)) for s in shifts
-        ]
-
-    mine = pl.ds(c * half + t * quarter, quarter)
-    theirs = pl.ds((1 - c) * half + t * quarter, quarter)
-    tok_y = net.put(tok.at[1 - c, pl.ds(t * quarter, quarter)], xs.at[mine], me.ctx)
-    small_o = whole(small, small_all)
-    q_o = whole(wq, wq_all)
-    o_o = whole(wo, wo_all)
-    cot_y = net.put(cot.at[1 - c, pl.ds(t * quarter, quarter)], gs.at[mine], me.ctx)
-    f_o = spread(wf, wf_all)
-    p_o = spread(wp, wp_all)
-    locals_ = [
-        own(tok.at[c], xs.at[pl.ds(c * half, half)], 0),
-        own(cot.at[c], gs.at[pl.ds(c * half, half)], 1),
-        own(small, small_all.at[d], 2),
-        own(wq, wq_all.at[d], 3),
-        own(wo, wo_all.at[d], 4),
-        own(wf, wf_all.at[d], 5),
-        own(wp, wp_all.at[d], 6),
-    ]
-
-    def relay(copies, dst):
-        out = []
-        for s, copy in zip(shifts, copies):
-            copy.wait_recv()
-            src = dst.at[me.from_outer(s)]
-            out.append(net.put(src, src, me.inner))
-        return out
-
-    rest = relay(small_o, small_all)
-    tok_y.wait_recv()
-    rest.append(net.put(xs.at[theirs], xs.at[theirs], me.tp))
-    rest += relay(q_o, wq_all)
-    rest += relay(o_o, wo_all)
-    cot_y.wait_recv()
-    rest.append(net.put(gs.at[theirs], gs.at[theirs], me.tp))
-    rest += [small_o[-1], q_o[-1], o_o[-1]]
-
-    def wide(copies, src, dst):
-        out, over = [], [net.put(src.at[pl.ds(c * hrow, hrow)], cut(dst, d), me.inner)]
-        for s, copy in zip(shifts, copies):
-            copy.wait_recv()
-            piece = cut(dst, me.from_outer(s))
-            over.append(net.put(piece, piece, me.inner))
-            out.append(net.put(piece, piece, me.ctx))
-        for s, copy in zip([0] + shifts, over):
-            copy.wait_recv()
-            piece = cut(dst, lax.rem(me.o + me.n_o - s, me.n_o) * 2 + 1 - me.i)
-            out.append(net.put(piece, piece, me.ctx))
-        return out
-
-    rest += wide(f_o, wf, wf_all)
-    rest += wide(p_o, wp, wp_all)
-    for copy in rest:
-        copy.wait_recv()
-    net.finish()
-    for copy in locals_:
-        copy.wait()
 
 
 def add_rows(dst, parts, rows, step):
@@ -268,80 +190,320 @@
     return pl.ds(pl.multiple_of(j * size, size), size)
 
 
+class Stage:
+    def __init__(self, me, net, src, dst, halves):
+        self.src, self.dst, self.halves, self.me = src, dst, halves, me
+        rows = dst.shape[1]
+        part = pl.ds(me.c * (rows // 2), rows // 2)
+
+        def cut(dev):
+            return dst.at[dev, part] if halves else dst.at[dev]
+
+        own = src.at[part] if halves else src
+        shifts = list(range(1, me.n_o))
+        self.outer = [net.make(own, cut(me.d), me.outer(s)) for s in shifts]
+        self.inner = [net.make(own, cut(me.d), me.inner)]
+        self.ctx = []
+        for s in shifts:
+            piece = cut(me.from_outer(s))
+            self.inner.append(net.make(piece, piece, me.inner))
+            if halves:
+                self.ctx.append(net.make(piece, piece, me.ctx))
+        self.far = []
+        if halves:
+            for s in [0] + shifts:
+                piece = cut(lax.rem(me.o + me.n_o - s, me.n_o) * 2 + 1 - me.i)
+                self.far.append(net.make(piece, piece, me.ctx))
+
+    def begin(self):
+        for copy in self.outer:
+            copy.start()
+
+    def begin_inner(self):
+        self.inner[0].start()
+
+    def relay(self, s):
+        self.outer[s].wait_recv()
+        self.inner[s + 1].start()
+        if self.halves:
+            self.ctx[s].start()
+
+    def cross(self, s):
+        self.inner[s].wait_recv()
+        self.far[s].start()
+
+    def arrive(self):
+        for copy in self.ctx + self.far if self.halves else self.inner:
+            copy.wait_recv()
+
+
+def placed(small_all, row, first, count, stride, offset, size):
+    lane = lax.broadcasted_iota(jnp.int32, (128, size), 0)
+    col = lax.broadcasted_iota(jnp.int32, (128, size), 1)
+    inside = (lane >= first) & (lane < first + count)
+
+    def add(d, total):
+        spot = inside & (col == lane - first + (d * stride + offset))
+        return total + lax.dot_general(
+            small_all[d, row : row + 8, :], spot.astype(F32), NN,
+            precision=lax.Precision.HIGHEST, preferred_element_type=F32,
+        )
+
+    return lax.fori_loop(0, small_all.shape[0], add, jnp.zeros((8, size), F32))
+
+
 def forward_kernel(
-    length, xs, vec, bq, bv, wq, wo, q, k, v, kt, h1t, o, ot, pt, part, vt
+    n_dp, direct, length, tok, cot, small, wq, wo, wf, wp,
+    vec, g_o, gt_o, x_o, h1t_o, q_o, k_o, v_o, kt_o, o_o, ot_o, pt_o, r1_o, a_o, sl_o, h2t_o,
+    wq_o, wo_o, wf_o, wp_o,
+    small_v, wq_v, wo_v, wf_v, x, gv, gm, gt, h1, h1t, q, k, v, kt, vt, o, ot, pt, ps, pr, r1, a, sl, h2t,
+    bias, fcb, send, recv, local, pts, rows_s,
 ):
-    rows, width = xs.shape
+    me = Place(n_dp, direct)
+    net = Net(send, recv)
+    d, c, t = me.d, me.c, me.t
+    rows, width = x.shape
     cols = q.shape[1]
-    step = 256
-
-    @pl.loop(0, rows // step)
-    def _(j):
-        at = block(j, step)
-        n, _ = norm(xs[at, :].astype(F32))
-        h1 = (n * vec[0:1, :] + vec[1:2, :]).astype(BF16)
-        h1t[:, at] = h1.T
-        proj = dot(h1, wq[...])
-        q[at, :] = (proj[:, :cols] + bq[...]).astype(BF16) * SCALE
+    half, step = rows // 2, 256
+    quarter = half // 2
+    shard = width // n_dp
+    n_blocks = rows // step
+    me.barrier()
+    done = []
+
+    def own(src, dst):
+        copy = pltpu.make_async_copy(src, dst, local.at[len(done)])
+        copy.start()
+        done.append(copy)
+        return copy
+
+    mine = pl.ds(c * half + t * quarter, quarter)
+    theirs = pl.ds((1 - c) * half + t * quarter, quarter)
+    first = net.take(n_blocks)
+
+    def exchange(j):
+        at = block(j, step)
+        return net.build(first + j, ps.at[at], pr.at[at], me.tp)
+
+    if direct:
+        tok_y = net.make(tok.at[1 - c, pl.ds(t * quarter, quarter)], x.at[mine], me.ctx)
+        tok_t = net.make(x.at[theirs], x.at[theirs], me.tp)
+        cot_y = net.make(cot.at[1 - c, pl.ds(t * quarter, quarter)], gv.at[mine], me.ctx)
+        cot_t = net.make(gv.at[theirs], gv.at[theirs], me.tp)
+        st_s = Stage(me, net, small, small_v, False)
+        st_q = Stage(me, net, wq, wq_v, True)
+        st_o = Stage(me, net, wo, wo_v, True)
+        st_f = Stage(me, net, wf, wf_v, True)
+        st_p = Stage(me, net, wp, wp_o, False)
+        tok_y.start()
+        st_s.begin()
+        st_s.begin_inner()
+        st_q.begin()
+        st_q.begin_inner()
+        st_o.begin()
+        st_o.begin_inner()
+        st_f.begin()
+        st_p.begin()
+        loads = [
+            own(tok.at[c], x.at[pl.ds(c * half, half)]),
+            own(cot.at[c], gv.at[pl.ds(c * half, half)]),
+            own(small, small_v.at[d]),
+            own(wq, wq_v.at[d]),
+            own(wo, wo_v.at[d]),
+            own(wf, wf_v.at[d]),
+        ]
+        own(wp, wp_o.at[d])
+        n_s = me.n_o - 1
+        for s in range(n_s):
+            st_s.relay(s)
+        tok_y.wait_recv()
+        tok_t.start()
+        for s in (0, 2, 1) if n_s == 3 else range(n_s):
+            st_q.relay(s)
+        cot_y.start()
+        st_s.arrive()
+        loads[2].wait()
+    else:
+        loads = [own(tok, x), own(cot, gv), own(small, small_v), own(wq, wq_v), own(wo, wo_v),
+                 own(wf, wf_v)]
+        own(wp, wp_o)
+        loads[2].wait()
+
+    vec[...] = placed(small_v, 0, 0, shard, shard, 0, width)
+    for s in range(2):
+        bias[8 * s : 8 * s + 8, :] = placed(
+            small_v, 6, s * (shard // 2), shard // 2, shard // 2, 0, cols
+        )
+    fcb[...] = placed(small_v, 7, 0, shard, 2 * shard, 0, fcb.shape[1])
+    fcb[0:1, :] = fcb[0:1, :] + placed(small_v, 8, 0, shard, 2 * shard, shard, fcb.shape[1])[0:1, :]
+    if direct:
+        for s in range(me.n_o):
+            st_q.cross(s)
+        for s in (0, 2, 1) if n_s == 3 else range(n_s):
+            st_o.relay(s)
+        tok_t.wait_recv()
+    loads[0].wait()
+
+    @pl.loop(0, n_blocks)
+    def _(j):
+        at = block(j, step)
+        n, _ = norm(x[at, :].astype(F32))
+        low = (n * vec[0:1, :] + vec[1:2, :]).astype(BF16)
+        h1[at, :] = low
+        h1t[:, at] = low.T
+
+    own(x, x_o)
+    own(h1t, h1t_o)
+    if direct:
+        for s in range(me.n_o):
+            st_o.cross(s)
+        st_f.begin_inner()
+        for s in (0, 2, 1) if n_s == 3 else range(n_s):
+            st_f.relay(s)
+        st_p.begin_inner()
+        st_q.arrive()
+    loads[3].wait()
+
+    @pl.loop(0, n_blocks)
+    def _(j):
+        at = block(j, step)
+        proj = dot(h1[at, :], wq_v[...].reshape(width, 3 * cols))
+        q[at, :] = (proj[:, :cols] + bias[0:1, :]).astype(BF16) * SCALE
         kk = proj[:, cols : 2 * cols].astype(BF16)
-        vv = (proj[:, 2 * cols :] + bv[...]).astype(BF16)
+        vv = (proj[:, 2 * cols :] + bias[8:9, :]).astype(BF16)
         k[at, :] = kk
         v[at, :] = vv
         kt[:, at] = kk.T
         vt[:, at] = vv.T
 
+    own(wq_v, wq_o)
+    for src, dst in ((q, q_o), (k, k_o), (v, v_o), (kt, kt_o)):
+        own(src, dst)
+    if direct:
+        for s in range(me.n_o):
+            st_f.cross(s)
+        cot_y.wait_recv()
+        cot_t.start()
+
     live = lax.broadcasted_iota(jnp.int32, (rows, step), 0) < length[0]
     side = lax.broadcasted_iota(jnp.int32, (step, 128), 1) // HD
 
-    @pl.loop(0, cols // 128)
-    def _(p):
-        pair = block(p, 128)
-
-        @pl.loop(0, rows // step)
-        def _(j):
-            at = block(j, step)
-            for hh in range(2):
-                qm = jnp.where(side == hh, q[at, pair], jnp.zeros((), BF16))
-                s = dot(k[:, pair], qm, NT)
-                s = jnp.where(live, s, NEG)
-                e = jnp.exp(s - jnp.max(s, axis=0, keepdims=True))
-                pb = (e * (1.0 / jnp.sum(e, axis=0, keepdims=True))).astype(BF16)
-                pt[p * 2 + hh, :, at] = pb
-                head = block(p * 2 + hh, HD)
-                ot[head, at] = dot(vt[head, :], pb).astype(BF16)
-
-    @pl.loop(0, rows // step)
+    def spill(slot, p, at):
+        return [
+            pltpu.make_async_copy(pt.at[slot, hh], pt_o.at[p * 2 + hh, :, at], pts.at[slot, hh])
+            for hh in range(2)
+        ]
+
+    steps = (cols // 128) * n_blocks
+
+    @pl.loop(0, steps)
+    def _(it):
+        p, j = it // n_blocks, it % n_blocks
+        pair, at, slot = block(p, 128), block(j, step), it % 2
+        if direct:
+            for s in range(n_s):
+
+                @pl.when(it == 2 + 3 * s if n_s == 3 else it == 2)
+                def _():
+                    st_p.relay(s)
+
+        @pl.when(it >= 2)
+        def _():
+            for copy in spill(slot, p, at):
+                copy.wait()
+
+        for hh in range(2):
+            qm = jnp.where(side == hh, q[at, pair], jnp.zeros((), BF16))
+            s = dot(k[:, pair], qm, NT)
+            s = jnp.where(live, s, NEG)
+            e = jnp.exp(s - jnp.max(s, axis=0, keepdims=True))
+            pb = (e * (1.0 / jnp.sum(e, axis=0, keepdims=True))).astype(BF16)
+            pt[slot, hh] = pb
+            head = block(p * 2 + hh, HD)
+            ot[head, at] = dot(vt[head, :], pb).astype(BF16)
+        for copy in spill(slot, p, at):
+            copy.start()
+
+    for slot in range(2):
+        for copy in spill(slot, 0, pl.ds(0, step)):
+            copy.wait()
+    own(ot, ot_o)
+    if direct:
+        st_o.arrive()
+    loads[4].wait()
+
+    @pl.loop(0, n_blocks)
     def _(j):
         at = block(j, step)
         ob = ot[:, at].T
         o[at, :] = ob
-        part[at, :] = dot(ob, wo[...], NT).astype(BF16)
-
-
-def mlp_kernel(
-    length, xs, gs, vec, bf, p0, p1, wf, wp, r1, a, du, h2t, gt, part2, part3
-):
-    rows, width = xs.shape
-    step = 256
-
-    @pl.loop(0, rows // step)
-    def _(j):
-        at = block(j, step)
-        mid = xs[at, :].astype(F32) + (p0[at, :].astype(F32) + p1[at, :].astype(F32)) + vec[2:3, :]
+        ps[at, :] = dot(ob, wo_v[...].reshape(width, cols), NT).astype(BF16)
+
+        @pl.when(j > 0)
+        def _():
+            exchange(j - 1).start()
+
+    own(wo_v, wo_o)
+    own(o, o_o)
+    exchange(n_blocks - 1).start()
+    if direct:
+        cot_t.wait_recv()
+        st_f.arrive()
+    loads[1].wait()
+    loads[5].wait()
+    own(wf_v, wf_o)
+
+    @pl.loop(0, n_blocks)
+    def _(j):
+        at = block(j, step)
+        on = j * step + lax.broadcasted_iota(jnp.int32, (step, width), 0) < length[0]
+        g = jnp.where(on, gv[at, :], jnp.zeros((), BF16))
+        gm[at, :] = g
+        gt[:, at] = g.T
+
+    own(gm, g_o)
+    own(gt, gt_o)
+
+    @pl.loop(0, n_blocks)
+    def _(j):
+        at = block(j, step)
+        exchange(j).wait_recv()
+        mid = x[at, :].astype(F32) + (ps[at, :].astype(F32) + pr[at, :].astype(F32)) + vec[2:3, :]
         r1[at, :] = mid
         n, _ = norm(mid)
         h2 = (n * vec[3:4, :] + vec[4:5, :]).astype(BF16)
         h2t[:, at] = h2.T
-        live = j * step + lax.broadcasted_iota(jnp.int32, (step, width), 0) < length[0]
-        g = jnp.where(live, gs[at, :], jnp.zeros((), BF16))
-        gt[:, at] = g.T
-        u = dot(h2, wf[...]) + bf[...]
+        u = dot(h2, wf_v[...].reshape(width, fcb.shape[1])) + fcb[0:1, :]
         s = jax.nn.sigmoid(GELU * u)
-        act = (u * s).astype(BF16)
-        a[at, :] = act
-        part2[at, :] = dot(act, wp[...], NT).astype(BF16)
-        slope = s * (1.0 + GELU * u * (1.0 - s))
-        dub = (dot(g, wp[...]) * slope).astype(BF16)
+        a[at, :] = (u * s).astype(BF16)
+        sl[at, :] = (s * (1.0 + GELU * u * (1.0 - s))).astype(BF16)
+        for n, (src, dst) in enumerate(((r1, r1_o), (a, a_o), (sl, sl_o))):
+            pltpu.make_async_copy(src.at[at], dst.at[at], rows_s.at[n, j]).start()
+
+    own(h2t, h2t_o)
+    if direct:
+        st_p.arrive()
+    net.finish()
+
+    @pl.loop(0, n_blocks)
+    def _(j):
+        at = block(j, step)
+        exchange(j).wait_send()
+        for n, (src, dst) in enumerate(((r1, r1_o), (a, a_o), (sl, sl_o))):
+            pltpu.make_async_copy(src.at[at], dst.at[at], rows_s.at[n, j]).wait()
+
+    for copy in done[6:]:
+        copy.wait()
+
+
+def mlp_kernel(g, a, sl, wf, wp, du, part2, part3):
+    step = 256
+
+    @pl.loop(0, g.shape[0] // step)
+    def _(j):
+        at = block(j, step)
+        part2[at, :] = dot(a[at, :], wp[...], NT).astype(BF16)
+        dub = (dot(g[at, :], wp[...]) * sl[at, :].astype(F32)).astype(BF16)
         du[at, :] = dub
         part3[at, :] = dot(dub, wf[...], NT).astype(BF16)
 
@@ -367,7 +529,7 @@
 
 
 def middle_kernel(
-    length, gs, vec, r1, p2a, p2b, p3a, p3b, o, wo, out, dr1, do, go, sums, dt
+    gs, vec, r1, p2a, p2b, p3a, p3b, o, wo, out, dr1, do, go, sums, dt
 ):
     rows, width = gs.shape
     step = 256
@@ -383,9 +545,7 @@
         n, inv = norm(mid)
         dh = p3a[at, :].astype(F32) + p3b[at, :].astype(F32)
         e = dh * vec[3:4, :]
-        live = j * step + lax.broadcasted_iota(jnp.int32, (step, width), 0) < length[0]
-        g = jnp.where(live, gs[at, :].astype(F32), 0.0)
-        grad = g + inv * (
+        grad = gs[at, :].astype(F32) + inv * (
             e - jnp.mean(e, axis=-1, keepdims=True) - n * jnp.mean(e * n, axis=-1, keepdims=True)
         )
         dr1[at, :] = grad
@@ -514,54 +674,49 @@
              qv_bias[:, :, 0].T.reshape(shard)] + list(fc_bias[:, 0].reshape(2, shard))
     small = jnp.pad(jnp.stack(lines), ((0, 16 - len(lines)), (0, 128 - shard)))
     wq_own = w_qkv.reshape(shard, 3 * cols)
-    if n_dp == 8:
-        outs = [((rows, width), BF16), ((rows, width), BF16), ((n_dp, 16, 128), F32),
-                ((n_dp, shard, 3 * cols), BF16), ((n_dp, shard, cols), BF16),
-                ((n_dp, shard, ff), BF16), ((n_dp, shard, ff), BF16)]
-        xs, gs, small_all, wq, wo, wf, wp = call(
-            functools.partial(gather_kernel, n_dp),
-            (tokens, cotangent, small, wq_own, w_out, w_fc, w_proj), outs,
-            [dma((64,)), dma((64,)), dma((7,))], [ANY] * 7, [ANY] * 7, "gather", 1)
+    direct = n_dp == 8
+    if direct:
+        ins = (length, tokens, cotangent, small, wq_own, w_out, w_fc, w_proj)
     else:
         def whole(a):
-            return lax.all_gather(a, "ctx", axis=1, tiled=True)
-
-        xs = lax.dynamic_index_in_dim(whole(tokens), ctx, 0, False)
-        gs = lax.dynamic_index_in_dim(whole(cotangent), ctx, 0, False)
-        small_all, wq, wo, wf, wp = [
-            lax.all_gather(a, "dp") for a in (small, wq_own, w_out, w_fc, w_proj)]
-    wq, wo, wf, wp = [a.reshape(n_dp * shard, -1) for a in (wq, wo, wf, wp)]
-    vec = small_all[:, :6, :shard].transpose(1, 0, 2).reshape(6, width)
-    vec = jnp.pad(vec, ((0, 2), (0, 0)))
-    qv = small_all[:, 6, :shard].reshape(n_dp, 2, shard // 2).transpose(1, 0, 2).reshape(2, cols)
-    bf = small_all[:, 7:9, :shard].reshape(1, ff)
-
+            return lax.dynamic_index_in_dim(
+                lax.all_gather(a, "ctx", axis=1, tiled=True), ctx, 0, False)
+
+        ins = (length, whole(tokens), whole(cotangent)) + tuple(
+            lax.all_gather(a, "dp") for a in (small, wq_own, w_out, w_fc, w_proj))
     act = ((rows, width), BF16)
+    act_t = ((width, rows), BF16)
     head = ((rows, cols), BF16)
     head_t = ((cols, rows), BF16)
-    q, k, v, kt, h1t, o, ot, pt, part1 = call(
-        forward_kernel, (length, xs, vec, qv[0:1], qv[1:2], wq, wo),
-        [head, head, head, head_t, ((width, rows), BF16), head, head_t,
-         ((cols // HD, rows, rows), BF16), act],
-        [pltpu.VMEM((cols, rows), BF16)], [SM] + [VM] * 6, name="forward")
+    wide = ((rows, ff), BF16)
+    mats = [((n_dp, shard, n), BF16) for n in (3 * cols, cols, ff, ff)]
+    outs = [((8, width), F32), act, act_t, act, act_t, head, head, head, head_t, head, head_t,
+            ((cols // HD, rows, rows), BF16), ((rows, width), F32), wide, wide, act_t] + mats
+    step = 256
+    held = [((n_dp, 16, 128), F32)] + mats[:3] + [
+        act, act, act, act_t, act, act_t, head, head, head, head_t, head_t, head, head_t,
+        ((2, 2, rows, step), BF16), act, act, ((rows, width), F32), wide, wide, act_t,
+        ((16, cols), F32), ((8, ff), F32)]
+    (vec, g, gt, xs, h1t, q, k, v, kt, o, ot, pt, r1, a, sl, h2t, wq, wo, wf, wp) = call(
+        functools.partial(forward_kernel, n_dp, direct), ins, outs,
+        [pltpu.VMEM(*h) for h in held]
+        + [dma((72,)), dma((72,)), dma((40,)), dma((2, 2)), dma((3, rows // step))],
+        [SM] + [ANY] * 7, [VM] + [ANY] * 19, "forward", 1)
+    wq, wo, wf, wp = [w.reshape(width, -1) for w in (wq, wo, wf, wp)]
 
     def other(a):
         return lax.ppermute(a, "tp", [(0, 1), (1, 0)])
 
-    r1, a, du, h2t, gt, part2, part3 = call(
-        mlp_kernel, (length, xs, gs, vec, bf, part1, other(part1), wf, wp),
-        [((rows, width), F32), ((rows, ff), BF16), ((rows, ff), BF16),
-         ((width, rows), BF16), ((width, rows), BF16), act, act],
-        specs=[SM] + [VM] * 8, name="mlp")
+    du, part2, part3 = call(mlp_kernel, (g, a, sl, wf, wp), [wide, act, act], name="mlp")
     gp, gf, bp, bfg = call(
         weights_kernel, (gt, h2t, a, du),
         [((width, ff), BF16), ((width, ff), BF16), ((1, width), F32), ((1, ff), F32)],
         name="weights")
     out_seq, dr1, do, go, sums2 = call(
         middle_kernel,
-        (length, gs, vec, r1, part2, other(part2), part3, other(part3), o, wo),
+        (g, vec, r1, part2, other(part2), part3, other(part3), o, wo),
         [act, ((rows, width), F32), head, ((width, cols), BF16), ((8, width), F32)],
-        [pltpu.VMEM((width, rows), BF16)], [SM] + [VM] * 9, name="middle")
+        [pltpu.VMEM((width, rows), BF16)], name="middle")
     gq, part4, sums3 = call(
         backward_kernel, (q, k, v, kt, h1t, ot, pt, do, wq),
         [((width, 3 * cols), BF16), act, ((8, 3 * cols), F32)],

time: 370 us -> 314 us (0.85)
  Pallas kernels: 331 us -> 283 us
  local copies, waits for them, and re-layouts: 27.1 us -> 21.5 us
    pallas_call x8 -> x7, Pallas kernels: 331 us -> 283 us  [call(): pl.pallas_call(body, out_shape=[jax.ShapeDtypeStruct(s, t) for s, t in ou...]
    ppermute x4 -> x3, waiting for transfers between devices: 7.45 us -> 5.36 us  [other(): return lax.ppermute(a, 'tp', [(0, 1), (1, 0)])]
    unnamed x27 -> x23, local copies, waits for them, and re-layouts: 9.69 us -> 8.61 us
  transfers between devices with their start and end apart: 4 -> 3, of which waited for: 3 -> 2; matrix products, arithmetic and copies ran while one was open for 1% -> 1% of each run, Pallas kernels for 4% -> 4%
where the time goes in v2:
time: 314 us; the launch traced here: 312 us
  Pallas kernels  283 us (90%)
  local copies, waits for them, and re-layouts  21.5 us (7%)
  waiting for transfers between devices  5.36 us (2%)
    pallas_call x7, Pallas kernels, call(): pl.pallas_call(body, out_shape=[jax.ShapeDtypeStruct(s, t) for s, t in ou...  283 us
    unnamed x23, local copies, waits for them, and re-layouts  8.61 us
  transfers between devices with their start and end apart: 3, of which 2 were waited for; matrix products, arithmetic and copies ran while one was open for 1% of the time, Pallas kernels for 4%

profile of v2, /device:TPU:0, one launch (start us, length us, event | category | flops | bytes accessed | tf_op | source)
XLA Modules:
  0.0 312.4 jit_solution(15442517932712266296)
XLA Ops:
  0.6 0.8 stack_reshape.3
  1.4 0.8 slice_bitcast_fusion.6
  2.2 1.6 copy.39
  3.9 1.2 dynamic_slice.3.length
  5.1 0.8 stack.30
  5.9 0.6 pad.8.small
  6.5 85.4 %forward.1 = (f32[8,768]{1,0:T(8,128)}, bf16[1024,768]{1,0:T(8,128)(2,1)}, bf16[768,1024]{1,0:T(8,128)(2,1)}, bf16[1024,768]{1,0:T(8,128)(2,1)}, bf16[768,1024]{...) custom-call(s32[1]{0:T(128)} %dynamic_slice.3.length, ...), custom_call_target="tpu_custom_call" | custom-call | tf_op jit(solution)/shard_map/forward/pallas_call | solution.py:652
  91.8 14.9 %mlp.1 = (bf16[1024,1536]{1,0:T(8,128)(2,1)}, bf16[1024,768]{1,0:T(8,128)(2,1)}, bf16[1024,768]{1,0:T(8,128)(2,1)}) custom-call(bf16[1024,768]{1,0:T(8,128)(2,1)} %get-tuple-element.65.g.gs, bf16[1024,1536]{1,0:T(8,128)(2,1)} %get-tuple-element.68.a, bf16[1024,1536]{1,0:T(8,128)(2,1)} %get-tuple-element.69.sl, bf16[768,1536]{1,0:T(8,128)(2,1)} %bitcast.52, ...), custom_call_target="tpu_custom_call" | custom-call | tf_op jit(solution)/shard_map/mlp/pallas_call | solution.py:652
  106.8 0.2 collective-permute-start
  107.0 0.3 collective-permute-start.1
  107.3 3.1 collective-permute-done.p2b
  110.4 0.0 copy-start.2
  110.4 2.2 collective-permute-done.1.p3b
  112.7 0.0 copy-done.2
  112.7 1.2 copy-done.3
  113.9 12.2 %middle.1 = (bf16[1024,768]{1,0:T(8,128)(2,1)}, f32[1024,768]{1,0:T(8,128)}, bf16[1024,384]{1,0:T(8,128)(2,1)}, bf16[768,384]{1,0:T(8,128)(2,1)}, f32[8,768]{1,0:T(8,128)}) custom-call(bf16[1024,768]{1,0:T(8,128)(2,1)} %get-tuple-element.65.g.gs, f32[8,768]{1,0:T(8,128)} %get-tuple-element.66.vec, f32[1024,768]{1,0:T(8,128)} %get-tuple-element.67.r1, ...), custom_call_target="tpu_custom_call" | custom-call | tf_op jit(solution)/shard_map/middle/pallas_call | solution.py:652
  126.1 34.5 %backward.1 = (bf16[768,1152]{1,0:T(8,128)(2,1)}, bf16[1024,768]{1,0:T(8,128)(2,1)}, f32[8,1152]{1,0:T(8,128)}) custom-call(bf16[1024,384]{1,0:T(8,128)(2,1)} %get-tuple-element.58.q, bf16[1024,384]{1,0:T(8,128)(2,1)} %get-tuple-element.59.k, bf16[1024,384]{1,0:T(8,128)(2,1)} %get-tuple-element.60.v, bf16[384,1024]{1,0:T(8,128)(2,1)} %get-tuple-element.61.kt, ...), custom_call_target="tpu_custom_call" | custom-call | tf_op jit(solution)/shard_map/backward/pallas_call | solution.py:652
  160.6 0.2 collective-permute-start.2
  160.8 13.1 %weights.1 = (bf16[768,1536]{1,0:T(8,128)(2,1)}, bf16[768,1536]{1,0:T(8,128)(2,1)}, f32[1,768]{1,0:T(1,128)}, f32[1,1536]{1,0:T(1,128)}) custom-call(bf16[768,1024]{1,0:T(8,128)(2,1)} %get-tuple-element.80.gt, bf16[768,1024]{1,0:T(8,128)(2,1)} %get-tuple-element.81.h2t, bf16[1024,1536]{1,0:T(8,128)(2,1)} %get-tuple-element.68.a, ...), custom_call_target="tpu_custom_call" | custom-call | tf_op jit(solution)/shard_map/weights/pallas_call | solution.py:652
  173.9 0.7 reduce.1
  174.6 0.1 reshape.87
  174.7 0.7 fusion
  175.4 0.1 reshape.85
  175.5 0.1 reshape.86
  175.6 0.0 copy-done.7
  175.6 0.0 collective-permute-done.2.pb
  175.6 0.0 copy-start.1
  175.7 1.1 copy-done.1
  176.8 7.2 %last.1 = (bf16[1024,768]{1,0:T(8,128)(2,1)}, f32[8,768]{1,0:T(8,128)}) custom-call(bf16[1024,768]{1,0:T(8,128)(2,1)} %get-tuple-element.85.xs, f32[8,768]{1,0:T(8,128)} %get-tuple-element.66.vec, f32[1024,768]{1,0:T(8,128)} %get-tuple-element.86.dr1, bf16[1024,768]{1,0:T(8,128)(2,1)} %get-tuple-element.87.pa, bf16[1024,768]{1,0:T(8,128)(2,1)} %copy-done.1), custom_call_target="tpu_custom_call" | custom-call | tf_op jit(solution)/shard_map/last/pallas_call | solution.py:652
  184.0 0.7 slice.38
  184.7 0.0 copy-done.8
  184.8 0.1 reshape.84
  184.9 0.7 select_maximum_fusion.small
  185.5 115.4 %reduce.6 = (f32[96,1152]{1,0:T(8,128)}, f32[96,384]{1,0:T(8,128)}, f32[96,1536]{1,0:T(8,128)}, f32[96,1536]{1,0:T(8,128)}, f32[16,128]{1,0:T(8,128)}, /*index=5...) custom-call(bf16[8,96,1152]{2,1,0:T(8,128)(2,1)} %bitcast.55, bf16[8,96,384]{2,1,0:T(8,128)(2,1)} %bitcast.57, ...), custom_call_target="tpu_custom_call" | custom-call | tf_op jit(solution)/shard_map/reduce/pallas_call | solution.py:652
  300.9 0.7 slice.48
  301.6 1.5 slice_bitcast_fusion
  303.1 0.6 reshape.89
  303.8 0.6 reshape_squeeze.4
  304.4 1.8 copy.43
  306.2 2.8 copy.51
  309.0 0.0 copy-done
  309.0 1.1 copy.52
  310.1 0.0 copy-done.6
  310.1 0.7 copy.53
  310.8 0.0 copy-done.5
  310.8 0.8 copy.54
  311.6 0.0 copy-done.4
  311.6 0.8 copy.55
  (12 shorter events, 0.1 us)
Async XLA Ops:
  106.8 3.6 %collective-permute-start = (bf16[1024,768]{1,0:T(8,128)(2,1)}, bf16[1024,768]{1,0:T(8,128)(2,1)S(1)}, u32[]{:S(2)}, u32[]{:S(2)}) collective-permute-start(bf16[1024,768]{1,0:T(8,128)(2,1)} %get-tuple-element.72.p2a), channel_id=1, source_target_pairs={{0,1},{1,0},{2,3},{3,2},{4,5},{5,4},{6,7},{7,6},{8,9},{9,8},{10,11... | collective-permute-start | bytes 4718600 | tf_op jit(solution)/shard_map/ppermute | solution.py:708
  107.0 5.7 %collective-permute-start.1 = (bf16[1024,768]{1,0:T(8,128)(2,1)}, bf16[1024,768]{1,0:T(8,128)(2,1)S(1)}, u32[]{:S(2)}, u32[]{:S(2)}) collective-permute-start(bf16[1024,768]{1,0:T(8,128)(2,1)} %get-tuple-element.73.p3a), channel_id=1, source_target_pairs={{0,1},{1,0},{2,3},{3,2},{4,5},{5,4},{6,7},{7,6},{8,9},{9,8},{10,11... | collective-permute-start | bytes 4718600 | tf_op jit(solution)/shard_map/ppermute | solution.py:708
  110.4 2.3 copy-start.2
  112.6 1.2 copy-start.3
  160.6 15.0 %collective-permute-start.2 = (bf16[1024,768]{1,0:T(8,128)(2,1)}, bf16[1024,768]{1,0:T(8,128)(2,1)S(1)}, u32[]{:S(2)}, u32[]{:S(2)}) collective-permute-start(bf16[1024,768]{1,0:T(8,128)(2,1)} %get-tuple-element.87.pa), channel_id=1, source_target_pairs={{0,1},{1,0},{2,3},{3,2},{4,5},{5,4},{6,7},{7,6},{8,9},{9,8},{10,11... | collective-permute-start | bytes 4718600 | tf_op jit(solution)/shard_map/ppermute | solution.py:708
  160.8 14.8 %copy-start.7 = (f32[8,768]{1,0:T(8,128)S(1)}, f32[8,768]{1,0:T(8,128)}, u32[]{:S(2)}) copy-start(f32[8,768]{1,0:T(8,128)} %get-tuple-element.89) | copy-start | bytes 73732
  175.6 1.1 copy-start.1
  176.8 8.0 %copy-start.8 = (f32[1,768]{1,0:T(1,128)S(1)}, f32[1,768]{1,0:T(1,128)}, u32[]{:S(2)}) copy-start(f32[1,768]{1,0:T(1,128)} %get-tuple-element.90) | copy-start | bytes 9220
  306.2 2.8 copy-start
  309.0 1.2 copy-start.6
  309.0 1.8 copy-start.5
  309.0 2.6 copy-start.4

commit v3 on v2

--- a/solution.py
+++ b/solution.py
@@ -15,7 +15,7 @@
 F32 = jnp.float32
 BF16 = jnp.bfloat16
 MESH = pl.DeviceIdType.MESH
-LIMIT = 60 * 2**20
+LIMIT = 67_000_000
 NN = (((1,), (0,)), ((), ()))
 NT = (((1,), (1,)), ((), ()))
 
@@ -80,11 +80,13 @@
     def tp(self):
         return (self.d, self.c, 1 - self.t)
 
-    def barrier(self):
+    def barrier(self, ctx=False):
         sem = pltpu.get_barrier_semaphore()
         peers = [self.tp]
+        if self.direct or ctx:
+            peers.append(self.ctx)
         if self.direct:
-            peers += [self.outer(s) for s in range(1, self.n_o)] + [self.inner, self.ctx]
+            peers += [self.outer(s) for s in range(1, self.n_o)] + [self.inner]
         for peer in peers:
             pl.semaphore_signal(sem, 1, device_id=peer, device_id_type=MESH)
         pl.semaphore_wait(sem, len(peers))
@@ -98,86 +100,6 @@
         for part in parts[1:]:
             total = total + part[at, :].astype(F32)
         dst[at, :] = total.astype(dst.dtype)
-
-
-def reduce_kernel(
-    n_dp, gq, go, gf, gp, small, out_seq, tok_seq,
-    rq, ro, rf, rp, rsmall, out, gtok,
-    xq, zq, sq, yq, xo, zo, so, yo, xf, zf, sf, yf, xp, zp, sp, yp, xm, zm, sm, ym,
-    send, recv, local,
-):
-    me = Place(n_dp)
-    net = Net(send, recv)
-    d, c, t = me.d, me.c, me.t
-    shifts = list(range(1, me.n_o))
-    half = out.shape[1]
-    quarter = half // 2
-    me.barrier()
-
-    mine = pl.ds((1 - c) * half + t * quarter, quarter)
-    final = []
-    seq_y = []
-    for src, dst in ((out_seq, out), (tok_seq, gtok)):
-        seq_y.append(net.put(src.at[mine], dst.at[c, pl.ds(t * quarter, quarter)], me.ctx))
-    locals_ = []
-    for k, (src, dst) in enumerate(((out_seq, out), (tok_seq, gtok))):
-        copy = pltpu.make_async_copy(src.at[pl.ds(c * half, half)], dst.at[c], local.at[k])
-        copy.start()
-        locals_.append(copy)
-
-    def outer_of(s):
-        return lax.rem(me.o + s, me.n_o)
-
-    def first(g, x):
-        return [
-            net.put(g.at[outer_of(s) * 2 + 1 - me.i], x.at[s], me.inner)
-            for s in shifts + [0]
-        ]
-
-    def second(g, x, z, sums, copies, rows, step):
-        out = []
-        for s, copy in zip(shifts + [0], copies):
-            copy.wait_recv()
-            add_rows(sums.at[s], [g.at[outer_of(s) * 2 + me.i], x.at[s]], rows, step)
-            if s:
-                out.append(net.put(sums.at[s], z.at[s - 1], me.outer(s)))
-        return out
-
-    def third(z, sums, y, copies, rows, step):
-        for copy in copies:
-            copy.wait_recv()
-        add_rows(y.at[0], [sums.at[0]] + [z.at[s - 1] for s in shifts], rows, step)
-        return net.put(y.at[0], y.at[1], me.ctx)
-
-    def fourth(y, r, copy, rows, step):
-        copy.wait_recv()
-        add_rows(r, [y.at[0], y.at[1]], rows, step)
-
-    groups = [
-        (gp, xp, zp, sp, yp, rp, 16),
-        (gf, xf, zf, sf, yf, rf, 16),
-        (go, xo, zo, so, yo, ro, 16),
-        (gq, xq, zq, sq, yq, rq, 16),
-        (small, xm, zm, sm, ym, rsmall, 8),
-    ]
-    ones = [first(g, x) for g, x, _, _, _, _, _ in groups]
-    twos = []
-    for copy, (src, dst) in zip(seq_y, ((out_seq, out), (tok_seq, gtok))):
-        copy.wait_recv()
-        place = dst.at[1 - c, pl.ds(t * quarter, quarter)]
-        final.append(net.put(place, place, me.tp))
-    for (g, x, z, s, y, r, step), copies in zip(groups, ones):
-        twos.append(second(g, x, z, s, copies, r.shape[0], step))
-    threes = []
-    for (g, x, z, s, y, r, step), copies in zip(groups, twos):
-        threes.append(third(z, s, y, copies, r.shape[0], step))
-    for (g, x, z, s, y, r, step), copy in zip(groups, threes):
-        fourth(y, r, copy, r.shape[0], step)
-    for copy in final:
-        copy.wait_recv()
-    net.finish()
-    for copy in locals_:
-        copy.wait()
 
 
 def norm(x):
@@ -496,148 +418,474 @@
         copy.wait()
 
 
-def mlp_kernel(g, a, sl, wf, wp, du, part2, part3):
-    step = 256
-
-    @pl.loop(0, g.shape[0] // step)
-    def _(j):
+def gather_lanes(dst, values, first, count, stride, offset):
+    size = values.shape[1]
+    lane = lax.broadcasted_iota(jnp.int32, (128, size), 0)
+    col = lax.broadcasted_iota(jnp.int32, (128, size), 1)
+    inside = (lane >= first) & (lane < first + count)
+
+    @pl.loop(0, dst.shape[0])
+    def _(d):
+        spot = inside & (col == lane - first + (d * stride + offset))
+        dst[d] += lax.dot_general(
+            values, spot.astype(F32), NT,
+            precision=lax.Precision.HIGHEST, preferred_element_type=F32,
+        )
+
+
+class Sum:
+    def __init__(self, me, net, g, x, z, y, step):
+        self.me, self.g, self.x, self.z, self.y, self.step = me, g, x, z, y, step
+        self.shifts = list(range(1, me.n_o))
+        self.order = self.shifts + [0]
+        self.one = {
+            s: net.make(g.at[self.at(s) * 2 + 1 - me.i], x.at[s], me.inner) for s in self.order
+        }
+        self.two = {
+            s: net.make(g.at[self.at(s) * 2 + me.i], z.at[s - 1], me.outer(s)) for s in self.shifts
+        }
+        self.three = net.make(g.at[me.d], y, me.ctx)
+
+    def at(self, s):
+        return lax.rem(self.me.o + s, self.me.n_o)
+
+    def begin(self):
+        for s in self.order:
+            self.one[s].start()
+
+    def add(self, s):
+        self.one[s].wait_recv()
+        part = self.g.at[self.at(s) * 2 + self.me.i]
+        add_rows(part, [part, self.x.at[s]], part.shape[0], self.step)
+        if s:
+            self.two[s].start()
+
+    def total(self):
+        for s in self.shifts:
+            self.two[s].wait_recv()
+        part = self.g.at[self.me.d]
+        add_rows(part, [part] + [self.z.at[s - 1] for s in self.shifts], part.shape[0], self.step)
+        self.three.start()
+
+    def final(self, write):
+        self.three.wait_recv()
+        part = self.g.at[self.me.d]
+
+        @pl.loop(0, part.shape[0] // self.step)
+        def _(j):
+            at = block(j, self.step)
+            write(at, part[at, :].astype(F32) + self.y[at, :].astype(F32))
+
+
+class SumCtx:
+    def __init__(self, me, net, g, y, x, z, w, step):
+        self.me, self.g, self.y, self.x, self.z, self.w, self.step = me, g, y, x, z, w, step
+        self.rows = g.shape[1] // 2
+        self.shifts = list(range(1, me.n_o))
+        self.order = self.shifts + [0]
+        self.mine = pl.ds(me.c * self.rows, self.rows)
+        other = pl.ds((1 - me.c) * self.rows, self.rows)
+        self.zero, self.zero_own = {}, {}
+        for s in self.order:
+            dev = self.at(s) * 2 + 1 - me.i
+            self.zero[s] = net.make(g.at[dev, other], y.at[dev], me.ctx)
+        for s in self.order:
+            dev = self.at(s) * 2 + me.i
+            self.zero_own[s] = net.make(g.at[dev, other], y.at[dev], me.ctx)
+        self.one = {
+            s: net.make(g.at[self.at(s) * 2 + 1 - me.i, self.mine], x.at[s], me.inner)
+            for s in self.order
+        }
+        self.two = {
+            s: net.make(g.at[self.at(s) * 2 + me.i, self.mine], z.at[s - 1], me.outer(s))
+            for s in self.shifts
+        }
+        self.three = net.make(g.at[me.d, self.mine], w, me.ctx)
+
+    at = Sum.at
+
+    def begin_row(self, s):
+        self.zero[s].start()
+        self.zero_own[s].start()
+
+    def cross(self, s):
+        self.zero[s].wait_recv()
+        dev = self.at(s) * 2 + 1 - self.me.i
+        part = self.g.at[dev, self.mine]
+        add_rows(part, [part, self.y.at[dev]], self.rows, self.step)
+        self.one[s].start()
+
+    def add(self, s):
+        self.zero_own[s].wait_recv()
+        self.one[s].wait_recv()
+        dev = self.at(s) * 2 + self.me.i
+        part = self.g.at[dev, self.mine]
+        add_rows(part, [part, self.y.at[dev], self.x.at[s]], self.rows, self.step)
+        if s:
+            self.two[s].start()
+
+    def total(self):
+        for s in self.shifts:
+            self.two[s].wait_recv()
+        part = self.g.at[self.me.d, self.mine]
+        add_rows(part, [part] + [self.z.at[s - 1] for s in self.shifts], self.rows, self.step)
+        self.three.start()
+
+    def final(self, write):
+        self.three.wait_recv()
+        part = self.g.at[self.me.d, self.mine]
+
+        @pl.loop(0, self.rows // self.step)
+        def _(j):
+            at = block(j, self.step)
+            here = pl.ds(pl.multiple_of(self.me.c * self.rows + j * self.step, self.step), self.step)
+            there = pl.ds(
+                pl.multiple_of((1 - self.me.c) * self.rows + j * self.step, self.step), self.step
+            )
+            write(here, part[at, :].astype(F32))
+            write(there, self.w[at, :].astype(F32))
+
+
+def backward_kernel(
+    n_dp, direct, vec, g_i, gt_i, x_i, h1t_i, q_i, k_i, v_i, kt_i, o_i, ot_i, pt_i, r1_i, a_i,
+    sl_i, h2t_i, wq_i, wo_i, wf_i, wp_i, *refs
+):
+    n_out = 7
+    out, gtok, rsmall, rq, ro, rf, rp = refs[:n_out]
+    (wq, wo, wf, wp, a, du, g, gt, ht, p2s, p2r, p3s, p3r, p4r, gp, gf, go, gq, small,
+     r1, o, do, dot_t, q, k, v, kt, ot, pt, dqt, dqkv, sums, low_sums, fcs, qvs) = refs[n_out : n_out + 35]
+    refs = refs[n_out + 35 :]
+    send, recv, local = refs[-3:]
+    buffers = refs[:-3]
+    me = Place(n_dp, direct)
+    net = Net(send, recv)
+    d, c, t = me.d, me.c, me.t
+    rows, width = g.shape
+    cols = q.shape[1]
+    ff = a.shape[1]
+    half, step = rows // 2, 256
+    quarter = half // 2
+    n_blocks = rows // step
+    groups, shard = gp.shape[0], gp.shape[1]
+    n_pairs = cols // 128
+    pending = []
+
+    def load(src, dst):
+        copy = pltpu.make_async_copy(src, dst, local.at[len(pending)])
+        copy.start()
+        pending.append(copy)
+        return copy
+
+    l_gt, l_a = load(gt_i, gt), load(a_i, a)
+    l_w = [load(wp_i, wp), load(wf_i, wf), load(g_i, g), load(sl_i, du)]
+    l_h2 = load(h2t_i, ht)
+    l_m = [load(r1_i, r1), load(wo_i, wo), load(o_i, o)]
+    l_b = [load(q_i, q), load(k_i, k), load(v_i, v), load(kt_i, kt), load(ot_i, ot), load(wq_i, wq)]
+    l_pt = load(pt_i.at[pl.ds(0, 2)], pt)
+    me.barrier(True)
+
+    def swap(first, src, dst, j):
         at = block(j, step)
-        part2[at, :] = dot(a[at, :], wp[...], NT).astype(BF16)
-        dub = (dot(g[at, :], wp[...]) * sl[at, :].astype(F32)).astype(BF16)
-        du[at, :] = dub
-        part3[at, :] = dot(dub, wf[...], NT).astype(BF16)
-
-
-def weights_kernel(gt, h2t, a, du, gp, gf, bp, bfg):
-    width = gt.shape[0]
-    step = 128
-
-    @pl.loop(0, width // step)
+        return net.build(first + j, src.at[at], dst.at[at], me.tp)
+
+    f2, f3, f4 = net.take(n_blocks), net.take(n_blocks), net.take(n_blocks)
+    ex2 = lambda j: swap(f2, p2s, p2r, j)
+    ex3 = lambda j: swap(f3, p3s, p3r, j)
+    ex4 = lambda j: swap(f4, p2s, p4r, j)
+    lead = (1 - c) * (n_blocks // 2) + t
+    mine = pl.ds((1 - c) * half + t * quarter, quarter)
+    there = pl.ds(t * quarter, quarter)
+    out_y = net.make(p2r.at[mine], out.at[c, there], me.ctx)
+    out_t = net.make(out.at[1 - c, there], out.at[1 - c, there], me.tp)
+    tok_y = net.make(p4r.at[mine], gtok.at[c, there], me.ctx)
+    tok_t = net.make(gtok.at[1 - c, there], gtok.at[1 - c, there], me.tp)
+
+    def write_to(ref):
+        def write(at, value):
+            ref[at, :] = value
+        return write
+
+    if direct:
+        b = list(buffers)
+        s_p = Sum(me, net, gp, b[0], b[1], b[2], 16)
+        s_f = SumCtx(me, net, gf, b[3], b[4], b[5], b[6], 16)
+        s_o = Sum(me, net, go, b[7], b[8], b[9], 16)
+        s_q = [
+            Sum(me, net, gq.at[p], b[10].at[p], b[11].at[p], b[12].at[p], 16)
+            for p in range(n_pairs)
+        ]
+        s_s = Sum(me, net, small, b[13], b[14], b[15], 8)
+        order = s_p.order
+    two = 2 * shard
+    n_z = width // two
+
+    def weight_rows(dst, lhs, rhs, each):
+        @pl.loop(0, n_z)
+        def _(s):
+            zz = lax.rem(me.o + 1 + s, n_z) if direct else s
+            value = dot(lhs[pl.ds(pl.multiple_of(zz * two, two), two), :], rhs)
+            value = value.astype(BF16).reshape(2, shard, value.shape[1])
+            dst[pl.ds(pl.multiple_of(zz * 2, 2), 2)] = value
+            if each is not None:
+                for n in range(n_z):
+
+                    @pl.when(s == n)
+                    def _():
+                        each((n + 1) % n_z)
+
+    l_gt.wait()
+    l_a.wait()
+    weight_rows(gp, gt, a[...], (lambda s: s_p.one[s].start()) if direct else None)
+    for copy in l_w:
+        copy.wait()
+
+    @pl.loop(0, n_blocks)
     def _(j):
         at = block(j, step)
-        gp[at, :] = dot(gt[at, :], a[...]).astype(BF16)
-        gf[at, :] = dot(h2t[at, :], du[...]).astype(BF16)
-
-    bp[...] = jnp.zeros_like(bp)
-    bfg[...] = jnp.zeros_like(bfg)
-
-    @pl.loop(0, du.shape[0] // 128)
-    def _(j):
-        at = block(j, 128)
-        bfg[...] += jnp.sum(du[at, :].astype(F32), axis=0, keepdims=True)
-        bp[...] += jnp.sum(gt[:, at].astype(F32).T, axis=0, keepdims=True)
-
-
-def middle_kernel(
-    gs, vec, r1, p2a, p2b, p3a, p3b, o, wo, out, dr1, do, go, sums, dt
-):
-    rows, width = gs.shape
-    step = 256
+        wp_all = wp[...].reshape(width, ff)
+        p2s[at, :] = dot(a[at, :], wp_all, NT).astype(BF16)
+        low = (dot(g[at, :], wp_all) * du[at, :].astype(F32)).astype(BF16)
+        du[at, :] = low
+
+        @pl.when(j > 0)
+        def _():
+            ex2(j - 1).start()
+            ex3(j - 1).start()
+
+        p3s[at, :] = dot(low, wf[...].reshape(width, ff), NT).astype(BF16)
+        fcs[0:1, :] = jnp.where(j == 0, 0.0, fcs[0:1, :]) + jnp.sum(
+            low.astype(F32), axis=0, keepdims=True
+        )
+
+    if direct:
+        s_p.add(1)
+    l_h2.wait()
+    ex2(n_blocks - 1).start()
+    ex3(n_blocks - 1).start()
+    weight_rows(gf, ht, du[...], s_f.begin_row if direct else None)
+    l_h1 = load(h1t_i, ht)
+    if direct:
+        s_p.add(2)
+    for copy in l_m:
+        copy.wait()
     sums[...] = jnp.zeros_like(sums)
 
-    @pl.loop(0, rows // step)
+    @pl.loop(0, n_blocks)
     def _(j):
         at = block(j, step)
+        ex2(j).wait_recv()
+        ex3(j).wait_recv()
         mid = r1[at, :]
-        out[at, :] = (
-            mid + (p2a[at, :].astype(F32) + p2b[at, :].astype(F32)) + vec[5:6, :]
+        p2r[at, :] = (
+            mid + (p2s[at, :].astype(F32) + p2r[at, :].astype(F32)) + vec[5:6, :]
         ).astype(BF16)
         n, inv = norm(mid)
-        dh = p3a[at, :].astype(F32) + p3b[at, :].astype(F32)
+        dh = p3s[at, :].astype(F32) + p3r[at, :].astype(F32)
         e = dh * vec[3:4, :]
-        grad = gs[at, :].astype(F32) + inv * (
+        gj = g[at, :].astype(F32)
+        grad = gj + inv * (
             e - jnp.mean(e, axis=-1, keepdims=True) - n * jnp.mean(e * n, axis=-1, keepdims=True)
         )
-        dr1[at, :] = grad
-        sums[0:1, :] += jnp.sum(grad, axis=0, keepdims=True)
-        sums[1:2, :] += jnp.sum(dh * n, axis=0, keepdims=True)
-        sums[2:3, :] += jnp.sum(dh, axis=0, keepdims=True)
+        r1[at, :] = grad
+        sums[2:3, :] += jnp.sum(grad, axis=0, keepdims=True)
+        sums[3:4, :] += jnp.sum(dh * n, axis=0, keepdims=True)
+        sums[4:5, :] += jnp.sum(dh, axis=0, keepdims=True)
+        sums[5:6, :] += jnp.sum(gj, axis=0, keepdims=True)
         gb = grad.astype(BF16)
-        dt[:, at] = gb.T
-        do[at, :] = dot(gb, wo[...]).astype(BF16)
-
-    @pl.loop(0, width // step)
-    def _(j):
-        at = block(j, step)
-        go[at, :] = dot(dt[at, :], o[...]).astype(BF16)
-
-
-def backward_kernel(
-    q, k, v, kt, h1t, ot, pt, do, wq, gq, part, sums, dot_t, dst, dqt, dqkv
-):
-    rows, cols = q.shape
-    step = 256
+        gt[:, at] = gb.T
+        dob = dot(gb, wo[...].reshape(width, cols)).astype(BF16)
+        do[at, :] = dob
+        dot_t[:, at] = dob.T
+
+    l_x = load(x_i, g)
+    own_out = load(p2r.at[pl.ds(c * half, half)], out.at[c])
+    if direct:
+        s_p.add(3)
+    weight_rows(go, gt, o[...], (lambda s: s_o.one[s].start()) if direct else None)
+    for copy in l_b:
+        copy.wait()
+    l_h1.wait()
     side = lax.broadcasted_iota(jnp.int32, (step, 128), 1) // HD
     side_all = lax.broadcasted_iota(jnp.int32, (rows, 128), 1) // HD
     zero = jnp.zeros((), BF16)
-
-    @pl.loop(0, rows // step)
-    def _(j):
-        at = block(j, step)
-        dot_t[:, at] = do[at, :].T
-
-    @pl.loop(0, cols // 128)
-    def _(p):
-        pair = block(p, 128)
+    dst = [a.at[:, pl.ds(0, rows)], du.at[:, pl.ds(0, rows)]]
+    events = [{}, {}, {}]
+    if direct:
+        events[0] = {
+            0: lambda: s_p.add(0),
+            1: lambda: s_f.cross(1),
+            2: lambda: s_f.cross(2),
+            3: lambda: s_o.add(1),
+            4: lambda: s_o.add(2),
+            5: lambda: s_f.cross(3),
+            6: lambda: s_o.add(3),
+            7: lambda: s_o.add(0),
+        }
+        events[1] = {
+            0: s_p.total,
+            1: lambda: s_f.cross(0),
+            2: out_y.start,
+            3: lambda: s_f.add(1),
+            5: lambda: s_f.add(2),
+            7: lambda: s_f.add(3),
+        }
+        events[2] = {
+            0: s_o.total,
+            1: lambda: s_f.add(0),
+            2: lambda: s_p.final(write_to(rp)),
+            4: lambda: s_q[0].add(1),
+            6: lambda: s_q[0].add(2),
+        }
+    else:
+        events[1] = {2: out_y.start}
+    for p in range(n_pairs):
+        pair = pl.ds(p * 128, 128)
+        l_pt.wait()
         for hh in range(2):
-            head = block(p * 2 + hh, HD)
-
-            @pl.loop(0, rows // step)
+            head = pl.ds((p * 2 + hh) * HD, HD)
+
+            @pl.loop(0, n_blocks)
             def _(j):
+                for n, event in events[p].items():
+                    if n // n_blocks == hh:
+
+                        @pl.when(j == n % n_blocks)
+                        def _():
+                            event()
+
                 at = block(j, step)
                 inner = jnp.sum(
                     dot_t[head, at].astype(F32) * ot[head, at].astype(F32), axis=0, keepdims=True
                 )
                 dp = dot(v[:, pair], jnp.where(side == hh, do[at, pair], zero), NT)
-                ds = (pt[p * 2 + hh, :, at].astype(F32) * (dp - inner)).astype(BF16)
-                dst[hh, :, at] = ds
-                dqt[head, at] = dot(kt[head, :], ds)
-
-        qp = q[:, pair]
-        dp_ = do[:, pair]
-        dk = dot(dst[0], jnp.where(side_all == 0, qp, zero)) + dot(
-            dst[1], jnp.where(side_all == 1, qp, zero)
+                ds = (pt[hh, :, at].astype(F32) * (dp - inner)).astype(BF16)
+                dst[hh][:, at] = ds
+                dqt[pl.ds(hh * HD, HD), at] = dot(kt[head, :], ds)
+
+        qp, dp_ = q[:, pair], do[:, pair]
+        dk = dot(dst[0][...], jnp.where(side_all == 0, qp, zero)) + dot(
+            dst[1][...], jnp.where(side_all == 1, qp, zero)
         )
-        dv = dot(pt[p * 2], jnp.where(side_all == 0, dp_, zero)) + dot(
-            pt[p * 2 + 1], jnp.where(side_all == 1, dp_, zero)
+        dv = dot(pt[0], jnp.where(side_all == 0, dp_, zero)) + dot(
+            pt[1], jnp.where(side_all == 1, dp_, zero)
         )
-        dqkv[:, pl.ds(pl.multiple_of(cols + p * 128, 128), 128)] = dk.astype(BF16)
-        dqkv[:, pl.ds(pl.multiple_of(2 * cols + p * 128, 128), 128)] = dv.astype(BF16)
-
-    sums[...] = jnp.zeros_like(sums)
-
-    @pl.loop(0, rows // step)
+        if p + 1 < n_pairs:
+            l_pt = load(pt_i.at[pl.ds(2 * p + 2, 2)], pt)
+        chunk = jnp.concatenate(
+            [(dqt[...].T * SCALE).astype(BF16), dk.astype(BF16), dv.astype(BF16)], axis=1
+        )
+        for n in range(3):
+            dqkv[:, pl.ds(n * cols + p * 128, 128)] = chunk[:, n * 128 : n * 128 + 128]
+        weight_rows(
+            gq.at[p], ht, chunk, (lambda s, p=p: s_q[p].one[s].start()) if direct else None
+        )
+
+    @pl.loop(0, n_blocks)
+    def _(j):
+        ex2(j).wait_send()
+
+    @pl.loop(0, n_blocks)
+    def _(j):
+        jj = lax.rem(lead + j, n_blocks)
+        at = block(jj, step)
+        p2s[at, :] = dot(dqkv[at, :], wq[...].reshape(width, 3 * cols), NT).astype(BF16)
+
+        @pl.when(j > 0)
+        def _():
+            ex4(lax.rem(lead + j - 1, n_blocks)).start()
+
+    qvs[...] = jnp.zeros_like(qvs)
+
+    @pl.loop(0, n_blocks)
     def _(j):
         at = block(j, step)
-        dqkv[at, 0:cols] = (dqt[:, at].T * SCALE).astype(BF16)
-        low = dqkv[at, :]
-        sums[0:1, :] += jnp.sum(low.astype(F32), axis=0, keepdims=True)
-        part[at, :] = dot(low, wq[...], NT).astype(BF16)
-
-    @pl.loop(0, h1t.shape[0] // step)
-    def _(j):
-        at = block(j, step)
-        gq[at, :] = dot(h1t[at, :], dqkv[...]).astype(BF16)
-
-
-def last_kernel(xs, vec, dr1, pa, pb, gtok, sums):
-    rows, width = xs.shape
-    step = 256
-    sums[...] = jnp.zeros_like(sums)
-
-    @pl.loop(0, rows // step)
-    def _(j):
-        at = block(j, step)
-        n, inv = norm(xs[at, :].astype(F32))
-        dh = pa[at, :].astype(F32) + pb[at, :].astype(F32)
+        qvs[0:1, :] += jnp.sum(dqkv[at, :].astype(F32), axis=0, keepdims=True)
+
+    ex4(lax.rem(lead + n_blocks - 1, n_blocks)).start()
+    l_x.wait()
+    if direct:
+        s_f.total()
+
+    @pl.loop(0, n_blocks)
+    def _(j):
+        jj = lax.rem(lead + j, n_blocks)
+        at = block(jj, step)
+        ex4(jj).wait_recv()
+        n, inv = norm(g[at, :].astype(F32))
+        dh = p2s[at, :].astype(F32) + p4r[at, :].astype(F32)
         e = dh * vec[0:1, :]
-        gtok[at, :] = (
-            dr1[at, :]
+        p4r[at, :] = (
+            r1[at, :]
             + inv
             * (e - jnp.mean(e, axis=-1, keepdims=True) - n * jnp.mean(e * n, axis=-1, keepdims=True))
         ).astype(BF16)
-        sums[0:1, :] += jnp.sum(dh * n, axis=0, keepdims=True)
-        sums[1:2, :] += jnp.sum(dh, axis=0, keepdims=True)
+        low_sums[pl.ds(jj, 1), :] = jnp.sum(dh * n, axis=0, keepdims=True)
+        low_sums[pl.ds(n_blocks + jj, 1), :] = jnp.sum(dh, axis=0, keepdims=True)
+
+        @pl.when(j == 1)
+        def _():
+            tok_y.start()
+
+    own_tok = load(p4r.at[pl.ds(c * half, half)], gtok.at[c])
+    for n in range(2):
+        sums[n : n + 1, :] = jnp.sum(
+            low_sums[n * n_blocks : (n + 1) * n_blocks, :], axis=0, keepdims=True
+        )
+    small[...] = jnp.zeros_like(small)
+    each = width // small.shape[0]
+    row = lax.broadcasted_iota(jnp.int32, (8, cols), 0)
+    wide_row = lax.broadcasted_iota(jnp.int32, (8, ff), 0)
+    top, low = small.at[:, pl.ds(0, 8)], small.at[:, pl.ds(8, 8)]
+    gather_lanes(top, sums[...], 0, each, each, 0)
+    for s in range(2):
+        part = qvs[0:1, pl.ds(2 * s * cols, cols)]
+        gather_lanes(top, jnp.where(row == 6, part, 0.0), s * (each // 2), each // 2, each // 2, 0)
+    fc = fcs[0:1, :]
+    gather_lanes(top, jnp.where(wide_row == 7, fc, 0.0), 0, each, 2 * each, 0)
+    gather_lanes(low, jnp.where(wide_row == 0, fc, 0.0), 0, each, 2 * each, each)
+    out_y.wait_recv()
+    out_t.start()
+    if direct:
+        s_s.begin()
+        s_q[0].add(3)
+        s_q[0].add(0)
+        for s in order:
+            s_q[1].add(s)
+        s_o.final(write_to(ro))
+        s_f.final(write_to(rf))
+        for s in order:
+            s_s.add(s)
+        for s in order:
+            s_q[2].add(s)
+        s_s.total()
+        for p in range(n_pairs):
+            s_q[p].total()
+    tok_y.wait_recv()
+    tok_t.start()
+    if direct:
+        s_s.final(write_to(rsmall))
+        for p in range(n_pairs):
+
+            def write(at, value, p=p):
+                for n in range(3):
+                    rq[at, pl.ds(n * cols + p * 128, 128)] = value[:, n * 128 : n * 128 + 128]
+
+            s_q[p].final(write)
+    else:
+        dumps = [load(gp, rp), load(gf, rf), load(go, ro), load(gq, rq), load(small, rsmall)]
+        for copy in dumps:
+            copy.wait()
+    out_t.wait_recv()
+    tok_t.wait_recv()
+
+    @pl.loop(0, n_blocks)
+    def _(j):
+        ex3(j).wait_send()
+        ex4(j).wait_send()
+
+    net.finish()
+    own_out.wait()
+    own_tok.wait()
 
 
 VM = pl.BlockSpec(memory_space=pltpu.VMEM)
@@ -702,64 +950,51 @@
         [pltpu.VMEM(*h) for h in held]
         + [dma((72,)), dma((72,)), dma((40,)), dma((2, 2)), dma((3, rows // step))],
         [SM] + [ANY] * 7, [VM] + [ANY] * 19, "forward", 1)
-    wq, wo, wf, wp = [w.reshape(width, -1) for w in (wq, wo, wf, wp)]
-
-    def other(a):
-        return lax.ppermute(a, "tp", [(0, 1), (1, 0)])
-
-    du, part2, part3 = call(mlp_kernel, (g, a, sl, wf, wp), [wide, act, act], name="mlp")
-    gp, gf, bp, bfg = call(
-        weights_kernel, (gt, h2t, a, du),
-        [((width, ff), BF16), ((width, ff), BF16), ((1, width), F32), ((1, ff), F32)],
-        name="weights")
-    out_seq, dr1, do, go, sums2 = call(
-        middle_kernel,
-        (g, vec, r1, part2, other(part2), part3, other(part3), o, wo),
-        [act, ((rows, width), F32), head, ((width, cols), BF16), ((8, width), F32)],
-        [pltpu.VMEM((width, rows), BF16)], name="middle")
-    gq, part4, sums3 = call(
-        backward_kernel, (q, k, v, kt, h1t, ot, pt, do, wq),
-        [((width, 3 * cols), BF16), act, ((8, 3 * cols), F32)],
-        [pltpu.VMEM((cols, rows), BF16), pltpu.VMEM((2, rows, rows), BF16),
-         pltpu.VMEM((cols, rows), F32), pltpu.VMEM((rows, 3 * cols), BF16)], name="backward")
-    tok_seq, sums1 = call(
-        last_kernel, (xs, vec, dr1, part4, other(part4)),
-        [act, ((8, width), F32)], name="last")
-
-    gvec = jnp.concatenate([sums1[0:2], sums2[0:3], bp])
-    gvec = gvec.reshape(6, n_dp, shard).transpose(1, 0, 2)
-    gqv = jnp.stack([sums3[0, :cols], sums3[0, 2 * cols :]]).reshape(2, n_dp, shard // 2)
-    gqv = gqv.transpose(1, 0, 2).reshape(n_dp, 1, shard)
-    gsmall = jnp.concatenate([gvec, gqv, bfg.reshape(n_dp, 2, shard)], axis=1)
-    gsmall = jnp.pad(gsmall, ((0, 0), (0, 7), (0, 128 - shard)))
-    gq, go, gf, gp = [a.reshape(n_dp, shard, -1) for a in (gq, go, gf, gp)]
-    if n_dp == 8:
-        n_o = n_dp // 2
-        scratch = []
-        for n, r, kind in ((3 * cols, shard, BF16), (cols, shard, BF16), (ff, shard, BF16),
-                           (ff, shard, BF16), (128, 16, F32)):
-            scratch += [pltpu.VMEM((n_o, r, n), kind), pltpu.VMEM((n_o - 1, r, n), kind),
-                        pltpu.VMEM((n_o, r, n), kind), pltpu.VMEM((2, r, n), kind)]
-        rq, ro, rf, rp, rs, out, gtok = call(
-            functools.partial(reduce_kernel, n_dp),
-            (gq, go, gf, gp, gsmall, out_seq, tok_seq),
-            [((shard, 3 * cols), F32), ((shard, cols), F32), ((shard, ff), F32),
-             ((shard, ff), F32), ((16, 128), F32), ((2, half, width), BF16),
-             ((2, half, width), BF16)],
-            scratch + [dma((64,)), dma((64,)), dma((2,))],
-            [VM] * 5 + [ANY] * 2, [VM] * 5 + [ANY] * 2, "reduce", 2)
+    groups = 8
+    part = width // groups
+    wq, wo, wf, wp = [w.reshape(groups, part, -1) for w in (wq, wo, wf, wp)]
+    n_pairs, n_o = cols // 128, n_dp // 2
+    narrow = 3 * 128
+    held = [(w.shape, BF16) for w in (wq, wo, wf, wp)] + [
+        wide, wide, act, act_t, act_t, act, act, act, act, act,
+        ((groups, part, ff), BF16), ((groups, part, ff), BF16), ((groups, part, cols), BF16),
+        ((n_pairs, groups, part, narrow), BF16), ((n_dp, 16, 128), F32),
+        ((rows, width), F32), head, head, head_t, head, head, head, head_t, head_t,
+        ((2, rows, rows), BF16), ((128, rows), F32), ((rows, 3 * cols), BF16),
+        ((8, width), F32), ((2 * rows // step, width), F32), ((8, ff), F32), ((8, 3 * cols), F32)]
+    seq = ((2, half, width), BF16)
+    if direct:
+        outs = [seq, seq, ((16, 128), F32), ((shard, 3 * cols), F32), ((shard, cols), F32),
+                ((shard, ff), F32), ((shard, ff), F32)]
+        hr = shard // 2
+        for n, lead, r, kind in ((ff, (), shard, BF16), (None, (), 0, BF16),
+                                 (cols, (), shard, BF16), (narrow, (n_pairs,), shard, BF16),
+                                 (128, (), 16, F32)):
+            if n is None:
+                held += [((n_dp, hr, ff), kind), ((n_o, hr, ff), kind),
+                         ((n_o - 1, hr, ff), kind), ((hr, ff), kind)]
+                continue
+            held += [(lead + (n_o, r, n), kind), (lead + (n_o - 1, r, n), kind),
+                     (lead + (r, n), kind)]
+        out_specs = [ANY] * 2 + [VM] * 5
     else:
+        outs = [seq, seq, ((n_dp, 16, 128), F32), ((n_pairs, groups, part, narrow), BF16),
+                ((groups, part, cols), BF16), ((groups, part, ff), BF16),
+                ((groups, part, ff), BF16)]
+        out_specs = [ANY] * 7
+    out, gtok, rs, rq, ro, rf, rp = call(
+        functools.partial(backward_kernel, n_dp, direct),
+        (vec, g, gt, xs, h1t, q, k, v, kt, o, ot, pt, r1, a, sl, h2t, wq, wo, wf, wp), outs,
+        [pltpu.VMEM(*h) for h in held] + [dma((96,)), dma((96,)), dma((40,))],
+        [VM] + [ANY] * 19, out_specs, "backward", 2)
+    if not direct:
         def summed(a):
-            return lax.psum(lax.psum_scatter(a, "dp", scatter_dimension=0), "ctx")
-
-        rq, ro, rf, rp = [summed(a).astype(F32) for a in (gq, go, gf, gp)]
-        rs = summed(gsmall)
-
-        def back(a):
-            pieces = lax.all_gather(a, "ctx", axis=0)
-            return lax.dynamic_slice(pieces, (0, ctx * half, 0), (2, half, width))
-
-        out, gtok = back(out_seq), back(tok_seq)
+            a = a.reshape(n_dp, shard, -1)
+            return lax.psum(lax.psum_scatter(a, "dp", scatter_dimension=0), "ctx").astype(F32)
+
+        rq = rq.reshape(n_pairs, width, 3, 128).transpose(1, 2, 0, 3).reshape(width, 3 * cols)
+        rq, ro, rf, rp = [summed(a) for a in (rq, ro, rf, rp)]
+        rs = lax.psum(lax.psum_scatter(rs, "dp", scatter_dimension=0), "ctx")
     line = [rs[j, :shard] for j in range(7)]
     return (out, gtok, line[0], line[1], rq.reshape(shard, 3, cols),
             line[6].reshape(2, shard // 2).T[:, :, None], ro, line[2], line[3], line[4],

time: 314 us -> 223 us (0.71)
  Pallas kernels: 283 us -> 204 us
  waiting for transfers between devices: 5.36 us -> 0 us
  local copies, waits for them, and re-layouts: 21.5 us -> 17.3 us
    pallas_call x7 -> x2, Pallas kernels: 283 us -> 204 us  [call(): pl.pallas_call(body, out_shape=[jax.ShapeDtypeStruct(s, t) for s, t in ou...]
    ppermute x3 -> x0, waiting for transfers between devices: 5.36 us -> none  [other(): return lax.ppermute(a, 'tp', [(0, 1), (1, 0)])]
    unnamed x23 -> x13, local copies, waits for them, and re-layouts: 8.61 us -> 6.22 us
  transfers between devices with their start and end apart: 3 -> 0, of which waited for: 2 -> 0; matrix products, arithmetic and copies ran while one was open for 1% -> 0% of each run, Pallas kernels for 4% -> 0%
where the time goes in v3:
time: 223 us; the launch traced here: 222 us
  Pallas kernels  204 us (91%)
  local copies, waits for them, and re-layouts  17.3 us (8%)
    pallas_call x2, Pallas kernels, call(): pl.pallas_call(body, out_shape=[jax.ShapeDtypeStruct(s, t) for s, t in ou...  204 us
    unnamed x13, local copies, waits for them, and re-layouts  6.22 us

profile of v3, /device:TPU:0, one launch (start us, length us, event | category | flops | bytes accessed | tf_op | source)
XLA Modules:
  0.0 222.2 jit_solution(14278568049294769712)
XLA Ops:
  0.6 1.2 dynamic_slice.3.length
  1.9 0.8 stack_reshape.3
  2.6 0.8 slice_bitcast_fusion.6
  3.5 0.8 stack.27
  4.2 0.6 pad.4.small
  4.8 1.6 copy.36
  6.5 85.3 %forward.1 = (f32[8,768]{1,0:T(8,128)}, bf16[1024,768]{1,0:T(8,128)(2,1)}, bf16[768,1024]{1,0:T(8,128)(2,1)}, bf16[1024,768]{1,0:T(8,128)(2,1)}, bf16[768,1024]{...) custom-call(s32[1]{0:T(128)} %dynamic_slice.3.length, ...), custom_call_target="tpu_custom_call" | custom-call | tf_op jit(solution)/shard_map/forward/pallas_call | solution.py:900
  91.8 118.9 %backward.1 = (bf16[2,512,768]{2,1,0:T(8,128)(2,1)}, bf16[2,512,768]{2,1,0:T(8,128)(2,1)}, f32[16,128]{1,0:T(8,128)}, f32[96,1152]{1,0:T(8,128)}, f32[96,384]{1,...) custom-call(f32[8,768]{1,0:T(8,128)} %get-tuple-element.41.vec, bf16[1024,768]{1,0:T(8,128)(2,1)} %get-tuple-element.42.g_i, ...), custom_call_target="tpu_custom_call" | custom-call | tf_op jit(solution)/shard_map/backward/pallas_call | solution.py:900
  210.7 0.7 slice.32
  211.4 1.5 slice_bitcast_fusion
  212.9 0.6 reshape.41
  213.6 0.6 reshape_squeeze.4
  214.2 1.8 copy.38
  216.0 0.0 copy-start
  216.0 2.8 %copy.44 = bf16[2,512,768]{2,1,0:T(8,128)(2,1)} copy(bf16[2,512,768]{2,1,0:T(8,128)(2,1)} %get-tuple-element.119) | data formatting | bytes 3145728
  218.8 0.0 copy-done
  218.8 0.0 copy-start.3
  218.8 0.0 copy-start.2
  218.8 0.0 copy-start.1
  218.8 1.1 copy.45
  219.9 0.0 copy-done.3
  219.9 0.7 copy.46
  220.6 0.0 copy-done.2
  220.6 0.8 copy.47
  221.4 0.0 copy-done.1
  221.4 0.8 copy.48
Async XLA Ops:
  216.0 2.8 %copy-start = (bf16[2,512,768]{2,1,0:T(8,128)(2,1)S(1)}, bf16[2,512,768]{2,1,0:T(8,128)(2,1)}, u32[]{:S(2)}) copy-start(bf16[2,512,768]{2,1,0:T(8,128)(2,1)} %get-tuple-element.120) | copy-start | bytes 4718596
  218.8 1.2 copy-start.3
  218.8 1.8 copy-start.2
  218.8 2.6 %copy-start.1 = (f32[96,1536]{1,0:T(8,128)S(1)}, f32[96,1536]{1,0:T(8,128)}, u32[]{:S(2)}) copy-start(f32[96,1536]{1,0:T(8,128)} %get-tuple-element.131) | copy-start | bytes 1769476

commit v4 on v3

--- a/solution.py
+++ b/solution.py
@@ -175,12 +175,15 @@
 
 
 def forward_kernel(
-    n_dp, direct, length, tok, cot, small, wq, wo, wf, wp,
+    n_dp, direct, length, tok, cot, *refs
+):
+    n_small = len(refs) - 56
+    lines, refs = refs[:n_small], refs[n_small:]
+    (wq, wo, wf, wp,
     vec, g_o, gt_o, x_o, h1t_o, q_o, k_o, v_o, kt_o, o_o, ot_o, pt_o, r1_o, a_o, sl_o, h2t_o,
     wq_o, wo_o, wf_o, wp_o,
-    small_v, wq_v, wo_v, wf_v, x, gv, gm, gt, h1, h1t, q, k, v, kt, vt, o, ot, pt, ps, pr, r1, a, sl, h2t,
-    bias, fcb, send, recv, local, pts, rows_s,
-):
+    small_s, small_v, wq_v, wo_v, wf_v, x, gv, gm, gt, h1, h1t, q, k, v, kt, vt, o, ot, pt, ps, pr, r1, a, sl, h2t,
+    bias, fcb, send, recv, local, pts, rows_s) = refs
     me = Place(n_dp, direct)
     net = Net(send, recv)
     d, c, t = me.d, me.c, me.t
@@ -190,7 +193,6 @@
     quarter = half // 2
     shard = width // n_dp
     n_blocks = rows // step
-    me.barrier()
     done = []
 
     def own(src, dst):
@@ -199,6 +201,21 @@
         done.append(copy)
         return copy
 
+    if direct:
+        ready = [own(wq.at[n], wq_v.at[d, :, pl.ds(n * cols, cols)]) for n in range(3)]
+        small_s[...] = jnp.zeros_like(small_s)
+        for n in range(6):
+            small_s[n : n + 1, 0:shard] = lines[n][...]
+        small_s[6:7, 0:shard] = jnp.concatenate([lines[6][0], lines[6][1]], axis=1)
+        for n in range(2):
+            small_s[7 + n : 8 + n, 0:shard] = lines[7][:, n * shard : (n + 1) * shard]
+        small_v[d] = small_s[...]
+        me.barrier()
+        for copy in ready:
+            copy.wait()
+    else:
+        me.barrier()
+    live_length = length[c]
     mine = pl.ds(c * half + t * quarter, quarter)
     theirs = pl.ds((1 - c) * half + t * quarter, quarter)
     first = net.take(n_blocks)
@@ -212,8 +229,8 @@
         tok_t = net.make(x.at[theirs], x.at[theirs], me.tp)
         cot_y = net.make(cot.at[1 - c, pl.ds(t * quarter, quarter)], gv.at[mine], me.ctx)
         cot_t = net.make(gv.at[theirs], gv.at[theirs], me.tp)
-        st_s = Stage(me, net, small, small_v, False)
-        st_q = Stage(me, net, wq, wq_v, True)
+        st_s = Stage(me, net, small_s, small_v, False)
+        st_q = Stage(me, net, wq_v.at[d], wq_v, True)
         st_o = Stage(me, net, wo, wo_v, True)
         st_f = Stage(me, net, wf, wf_v, True)
         st_p = Stage(me, net, wp, wp_o, False)
@@ -226,14 +243,13 @@
         st_o.begin_inner()
         st_f.begin()
         st_p.begin()
-        loads = [
+        l_x, l_g, l_o, l_f = [
             own(tok.at[c], x.at[pl.ds(c * half, half)]),
             own(cot.at[c], gv.at[pl.ds(c * half, half)]),
-            own(small, small_v.at[d]),
-            own(wq, wq_v.at[d]),
             own(wo, wo_v.at[d]),
             own(wf, wf_v.at[d]),
         ]
+        first_out = len(done)
         own(wp, wp_o.at[d])
         n_s = me.n_o - 1
         for s in range(n_s):
@@ -244,12 +260,13 @@
             st_q.relay(s)
         cot_y.start()
         st_s.arrive()
-        loads[2].wait()
     else:
-        loads = [own(tok, x), own(cot, gv), own(small, small_v), own(wq, wq_v), own(wo, wo_v),
-                 own(wf, wf_v)]
+        ready = [own(lines[0], small_v), own(wq, wq_v)]
+        l_x, l_g, l_o, l_f = own(tok, x), own(cot, gv), own(wo, wo_v), own(wf, wf_v)
+        first_out = len(done)
         own(wp, wp_o)
-        loads[2].wait()
+        for copy in ready:
+            copy.wait()
 
     vec[...] = placed(small_v, 0, 0, shard, shard, 0, width)
     for s in range(2):
@@ -264,7 +281,7 @@
         for s in (0, 2, 1) if n_s == 3 else range(n_s):
             st_o.relay(s)
         tok_t.wait_recv()
-    loads[0].wait()
+    l_x.wait()
 
     @pl.loop(0, n_blocks)
     def _(j):
@@ -284,7 +301,6 @@
             st_f.relay(s)
         st_p.begin_inner()
         st_q.arrive()
-    loads[3].wait()
 
     @pl.loop(0, n_blocks)
     def _(j):
@@ -307,7 +323,7 @@
         cot_y.wait_recv()
         cot_t.start()
 
-    live = lax.broadcasted_iota(jnp.int32, (rows, step), 0) < length[0]
+    live = lax.broadcasted_iota(jnp.int32, (rows, step), 0) < live_length
     side = lax.broadcasted_iota(jnp.int32, (step, 128), 1) // HD
 
     def spill(slot, p, at):
@@ -352,7 +368,7 @@
     own(ot, ot_o)
     if direct:
         st_o.arrive()
-    loads[4].wait()
+    l_o.wait()
 
     @pl.loop(0, n_blocks)
     def _(j):
@@ -371,14 +387,14 @@
     if direct:
         cot_t.wait_recv()
         st_f.arrive()
-    loads[1].wait()
-    loads[5].wait()
+    l_g.wait()
+    l_f.wait()
     own(wf_v, wf_o)
 
     @pl.loop(0, n_blocks)
     def _(j):
         at = block(j, step)
-        on = j * step + lax.broadcasted_iota(jnp.int32, (step, width), 0) < length[0]
+        on = j * step + lax.broadcasted_iota(jnp.int32, (step, width), 0) < live_length
         g = jnp.where(on, gv[at, :], jnp.zeros((), BF16))
         gm[at, :] = g
         gt[:, at] = g.T
@@ -414,7 +430,7 @@
         for n, (src, dst) in enumerate(((r1, r1_o), (a, a_o), (sl, sl_o))):
             pltpu.make_async_copy(src.at[at], dst.at[at], rows_s.at[n, j]).wait()
 
-    for copy in done[6:]:
+    for copy in done[first_out:]:
         copy.wait()
 
 
@@ -551,12 +567,16 @@
     sl_i, h2t_i, wq_i, wo_i, wf_i, wp_i, *refs
 ):
     n_out = 7
-    out, gtok, rsmall, rq, ro, rf, rp = refs[:n_out]
+    out, gtok, rsmall, rq_o, ro_o, rf_o, rp_o = refs[:n_out]
     (wq, wo, wf, wp, a, du, g, gt, ht, p2s, p2r, p3s, p3r, p4r, gp, gf, go, gq, small,
      r1, o, do, dot_t, q, k, v, kt, ot, pt, dqt, dqkv, sums, low_sums, fcs, qvs) = refs[n_out : n_out + 35]
     refs = refs[n_out + 35 :]
     send, recv, local = refs[-3:]
     buffers = refs[:-3]
+    if direct:
+        (rq, ro, rf, rp), buffers = buffers[:4], buffers[4:]
+    else:
+        rq, ro, rf, rp = rq_o, ro_o, rf_o, rp_o
     me = Place(n_dp, direct)
     net = Net(send, recv)
     d, c, t = me.d, me.c, me.t
@@ -705,6 +725,11 @@
     for copy in l_b:
         copy.wait()
     l_h1.wait()
+    copy_p = pltpu.make_async_copy(rp, rp_o, local.at[39]) if direct else None
+
+    def send_p():
+        copy_p.start()
+
     side = lax.broadcasted_iota(jnp.int32, (step, 128), 1) // HD
     side_all = lax.broadcasted_iota(jnp.int32, (rows, 128), 1) // HD
     zero = jnp.zeros((), BF16)
@@ -733,6 +758,7 @@
             0: s_o.total,
             1: lambda: s_f.add(0),
             2: lambda: s_p.final(write_to(rp)),
+            3: send_p,
             4: lambda: s_q[0].add(1),
             6: lambda: s_q[0].add(2),
         }
@@ -852,7 +878,9 @@
         for s in order:
             s_q[1].add(s)
         s_o.final(write_to(ro))
+        results = [load(ro, ro_o)]
         s_f.final(write_to(rf))
+        results.append(load(rf, rf_o))
         for s in order:
             s_s.add(s)
         for s in order:
@@ -868,9 +896,10 @@
 
             def write(at, value, p=p):
                 for n in range(3):
-                    rq[at, pl.ds(n * cols + p * 128, 128)] = value[:, n * 128 : n * 128 + 128]
+                    rq[n, at, pl.ds(p * 128, 128)] = value[:, n * 128 : n * 128 + 128]
 
             s_q[p].final(write)
+        results.append(load(rq, rq_o))
     else:
         dumps = [load(gp, rp), load(gf, rf), load(go, ro), load(gq, rq), load(small, rsmall)]
         for copy in dumps:
@@ -886,6 +915,35 @@
     net.finish()
     own_out.wait()
     own_tok.wait()
+    if direct:
+        copy_p.wait()
+        for copy in results:
+            copy.wait()
+
+
+def finish_kernel(shard, small, *refs):
+    big_i, refs = refs[:6], refs[6:]
+    big_o, (lines_o, qv_o, fc_o), refs = refs[:6], (refs[6:12], refs[12], refs[13]), refs[14:]
+    buffers, sem_i, sem_o = refs[:6], refs[6], refs[7]
+    parts = []
+    for n, (src, dst, buf) in enumerate(zip(big_i, big_o, buffers)):
+        count = src.shape[0] if len(src.shape) == 3 else 1
+        for k in range(count):
+            at = (lambda r, k=k: r.at[k]) if len(src.shape) == 3 else (lambda r: r)
+            load = pltpu.make_async_copy(at(src), at(buf), sem_i.at[len(parts)])
+            store = pltpu.make_async_copy(at(buf), at(dst), sem_o.at[len(parts)])
+            load.start()
+            parts.append((load, store))
+    for n in range(6):
+        lines_o[n][...] = small[n : n + 1, 0:shard]
+    for n in range(2):
+        qv_o[n] = small[6:7, n * (shard // 2) : (n + 1) * (shard // 2)]
+        fc_o[:, n * shard : (n + 1) * shard] = small[7 + n : 8 + n, 0:shard]
+    for load, store in parts:
+        load.wait()
+        store.start()
+    for _, store in parts:
+        store.wait()
 
 
 VM = pl.BlockSpec(memory_space=pltpu.VMEM)
@@ -916,21 +974,23 @@
     cols = w_out.shape[1]
     ff = w_fc.shape[1]
     dma = pltpu.SemaphoreType.DMA
-    ctx = lax.axis_index("ctx")
-    length = lax.dynamic_slice(lengths, (ctx,), (1,))
-    lines = [ln1_gain, ln1_bias, out_bias, ln2_gain, ln2_bias, proj_bias,
-             qv_bias[:, :, 0].T.reshape(shard)] + list(fc_bias[:, 0].reshape(2, shard))
-    small = jnp.pad(jnp.stack(lines), ((0, 16 - len(lines)), (0, 128 - shard)))
-    wq_own = w_qkv.reshape(shard, 3 * cols)
     direct = n_dp == 8
-    if direct:
-        ins = (length, tokens, cotangent, small, wq_own, w_out, w_fc, w_proj)
+    lines = [ln1_gain, ln1_bias, out_bias, ln2_gain, ln2_bias, proj_bias]
+    if direct:
+        ins = [lengths, tokens, cotangent] + [a[None] for a in lines] + [
+            qv_bias.transpose(1, 2, 0), fc_bias.T, w_qkv.transpose(1, 0, 2), w_out, w_fc, w_proj]
+        specs = [SM, ANY, ANY] + [VM] * 8 + [ANY] * 4
     else:
+        lines = lines + [qv_bias[:, :, 0].T.reshape(shard)] + list(fc_bias[:, 0].reshape(2, shard))
+        small = jnp.pad(jnp.stack(lines), ((0, 16 - len(lines)), (0, 128 - shard)))
+        wq_own = w_qkv.reshape(shard, 3 * cols)
+        specs = [SM] + [ANY] * 7
+
         def whole(a):
             return lax.dynamic_index_in_dim(
-                lax.all_gather(a, "ctx", axis=1, tiled=True), ctx, 0, False)
-
-        ins = (length, whole(tokens), whole(cotangent)) + tuple(
+                lax.all_gather(a, "ctx", axis=1, tiled=True), lax.axis_index("ctx"), 0, False)
+
+        ins = (lengths, whole(tokens), whole(cotangent)) + tuple(
             lax.all_gather(a, "dp") for a in (small, wq_own, w_out, w_fc, w_proj))
     act = ((rows, width), BF16)
     act_t = ((width, rows), BF16)
@@ -941,7 +1001,7 @@
     outs = [((8, width), F32), act, act_t, act, act_t, head, head, head, head_t, head, head_t,
             ((cols // HD, rows, rows), BF16), ((rows, width), F32), wide, wide, act_t] + mats
     step = 256
-    held = [((n_dp, 16, 128), F32)] + mats[:3] + [
+    held = [((16, 128), F32), ((n_dp, 16, 128), F32)] + mats[:3] + [
         act, act, act, act_t, act, act_t, head, head, head, head_t, head_t, head, head_t,
         ((2, 2, rows, step), BF16), act, act, ((rows, width), F32), wide, wide, act_t,
         ((16, cols), F32), ((8, ff), F32)]
@@ -949,7 +1009,7 @@
         functools.partial(forward_kernel, n_dp, direct), ins, outs,
         [pltpu.VMEM(*h) for h in held]
         + [dma((72,)), dma((72,)), dma((40,)), dma((2, 2)), dma((3, rows // step))],
-        [SM] + [ANY] * 7, [VM] + [ANY] * 19, "forward", 1)
+        specs, [VM] + [ANY] * 19, "forward", 1)
     groups = 8
     part = width // groups
     wq, wo, wf, wp = [w.reshape(groups, part, -1) for w in (wq, wo, wf, wp)]
@@ -964,8 +1024,9 @@
         ((8, width), F32), ((2 * rows // step, width), F32), ((8, ff), F32), ((8, 3 * cols), F32)]
     seq = ((2, half, width), BF16)
     if direct:
-        outs = [seq, seq, ((16, 128), F32), ((shard, 3 * cols), F32), ((shard, cols), F32),
-                ((shard, ff), F32), ((shard, ff), F32)]
+        big = [((3, shard, cols), F32), ((shard, cols), F32), ((shard, ff), F32), ((shard, ff), F32)]
+        outs = [seq, seq, ((16, 128), F32)] + big
+        held += big
         hr = shard // 2
         for n, lead, r, kind in ((ff, (), shard, BF16), (None, (), 0, BF16),
                                  (cols, (), shard, BF16), (narrow, (n_pairs,), shard, BF16),
@@ -976,7 +1037,7 @@
                 continue
             held += [(lead + (n_o, r, n), kind), (lead + (n_o - 1, r, n), kind),
                      (lead + (r, n), kind)]
-        out_specs = [ANY] * 2 + [VM] * 5
+        out_specs = [ANY] * 2 + [VM] + [ANY] * 4
     else:
         outs = [seq, seq, ((n_dp, 16, 128), F32), ((n_pairs, groups, part, narrow), BF16),
                 ((groups, part, cols), BF16), ((groups, part, ff), BF16),
@@ -995,6 +1056,15 @@
         rq = rq.reshape(n_pairs, width, 3, 128).transpose(1, 2, 0, 3).reshape(width, 3 * cols)
         rq, ro, rf, rp = [summed(a) for a in (rq, ro, rf, rp)]
         rs = lax.psum(lax.psum_scatter(rs, "dp", scatter_dimension=0), "ctx")
+    if direct:
+        mats = [seq, seq] + big
+        small = [((1, shard), F32)] * 6 + [((2, 1, shard // 2), F32), ((1, 2 * shard), F32)]
+        (out, gtok, rq, ro, rf, rp, g1, b1, bo, g2, b2, bp, qv, fc) = call(
+            functools.partial(finish_kernel, shard), (rs, out, gtok, rq, ro, rf, rp), mats + small,
+            [pltpu.VMEM(*m) for m in mats] + [dma((12,)), dma((12,))],
+            [VM] + [ANY] * 6, [ANY] * 6 + [VM] * 8, "finish")
+        return (out, gtok, g1[0], b1[0], rq.transpose(1, 0, 2), qv.transpose(2, 0, 1), ro, bo[0],
+                g2[0], b2[0], rf, fc.T, rp, bp[0])
     line = [rs[j, :shard] for j in range(7)]
     return (out, gtok, line[0], line[1], rq.reshape(shard, 3, cols),
             line[6].reshape(2, shard // 2).T[:, :, None], ro, line[2], line[3], line[4],

time: 223 us -> 211 us (0.946)
  local copies, waits for them, and re-layouts: 17.3 us -> 0 us
  Pallas kernels: 204 us -> 210 us
    unnamed x13 -> x0, local copies, waits for them, and re-layouts: 6.22 us -> none
    pallas_call x2 -> x3, Pallas kernels: 204 us -> 210 us  [call(): pl.pallas_call(body, out_shape=[jax.ShapeDtypeStruct(s, t) for s, t in ou...]
    reshape x3 -> x0, local copies, waits for them, and re-layouts: 4.09 us -> none  [the longest x1 1.8 us: on_device(): rq.reshape(shard, 3, cols)]
    another operation x4 -> x0, local copies, waits for them, and re-layouts: 2.97 us -> none  [the longest x2 1.53 us: on_device(): small = jnp.pad(jnp.stack(lines), ((0, 16 - len(lines)), (0, 128 - shard)))]
where the time goes in v4:
time: 211 us
  Pallas kernels  210 us (100%)
    pallas_call x3, Pallas kernels, call(): pl.pallas_call(body, out_shape=[jax.ShapeDtypeStruct(s, t) for s, t in ou...  210 us

profile of v4, /device:TPU:0, one launch (start us, length us, event | category | flops | bytes accessed | tf_op | source)
XLA Modules:
  0.0 210.7 jit_solution(10874690548732389839)
XLA Ops:
  0.7 85.5 %forward.1 = (f32[8,768]{1,0:T(8,128)}, bf16[1024,768]{1,0:T(8,128)(2,1)}, bf16[768,1024]{1,0:T(8,128)(2,1)}, bf16[1024,768]{1,0:T(8,128)(2,1)}, bf16[768,1024]{...) custom-call(s32[2]{0:T(128)} %length.1, ...), custom_call_target="tpu_custom_call" | custom-call | tf_op jit(solution)/shard_map/forward/pallas_call | solution.py:958
  86.1 118.9 %backward.1 = (bf16[2,512,768]{2,1,0:T(8,128)(2,1)}, bf16[2,512,768]{2,1,0:T(8,128)(2,1)}, f32[16,128]{1,0:T(8,128)}, f32[3,96,384]{2,1,0:T(8,128)}, f32[96,384]...) custom-call(f32[8,768]{1,0:T(8,128)} %get-tuple-element.55.vec, bf16[1024,768]{1,0:T(8,128)(2,1)} %get-tuple-element.56.g_i, ...), custom_call_target="tpu_custom_call" | custom-call | tf_op jit(solution)/shard_map/backward/pallas_call | solution.py:958
  205.0 5.5 %finish.1 = (bf16[2,512,768]{2,1,0:T(8,128)(2,1)}, bf16[2,512,768]{2,1,0:T(8,128)(2,1)}, f32[3,96,384]{2,1,0:T(8,128)}, f32[96,384]{1,0:T(8,128)}, f32[96,1536]{...) custom-call(f32[16,128]{1,0:T(8,128)} %get-tuple-element.75.small, ...), custom_call_target="tpu_custom_call" | custom-call | tf_op jit(solution)/shard_map/finish/pallas_call | solution.py:958

commit v5 on v4

--- a/solution.py
+++ b/solution.py
@@ -760,7 +760,9 @@
             2: lambda: s_p.final(write_to(rp)),
             3: send_p,
             4: lambda: s_q[0].add(1),
-            6: lambda: s_q[0].add(2),
+            5: lambda: s_q[0].add(2),
+            6: lambda: s_q[0].add(3),
+            7: lambda: s_q[0].add(0),
         }
     else:
         events[1] = {2: out_y.start}
@@ -831,6 +833,19 @@
     l_x.wait()
     if direct:
         s_f.total()
+        for s in order:
+            s_q[1].add(s)
+    small[...] = jnp.zeros_like(small)
+    each = width // small.shape[0]
+    row = lax.broadcasted_iota(jnp.int32, (8, cols), 0)
+    wide_row = lax.broadcasted_iota(jnp.int32, (8, ff), 0)
+    top, low = small.at[:, pl.ds(0, 8)], small.at[:, pl.ds(8, 8)]
+    for s in range(2):
+        part = qvs[0:1, pl.ds(2 * s * cols, cols)]
+        gather_lanes(top, jnp.where(row == 6, part, 0.0), s * (each // 2), each // 2, each // 2, 0)
+    fc = fcs[0:1, :]
+    gather_lanes(top, jnp.where(wide_row == 7, fc, 0.0), 0, each, 2 * each, 0)
+    gather_lanes(low, jnp.where(wide_row == 0, fc, 0.0), 0, each, 2 * each, each)
 
     @pl.loop(0, n_blocks)
     def _(j):
@@ -857,37 +872,24 @@
         sums[n : n + 1, :] = jnp.sum(
             low_sums[n * n_blocks : (n + 1) * n_blocks, :], axis=0, keepdims=True
         )
-    small[...] = jnp.zeros_like(small)
-    each = width // small.shape[0]
-    row = lax.broadcasted_iota(jnp.int32, (8, cols), 0)
-    wide_row = lax.broadcasted_iota(jnp.int32, (8, ff), 0)
-    top, low = small.at[:, pl.ds(0, 8)], small.at[:, pl.ds(8, 8)]
+    if direct:
+        for s in order:
+            s_q[2].add(s)
     gather_lanes(top, sums[...], 0, each, each, 0)
-    for s in range(2):
-        part = qvs[0:1, pl.ds(2 * s * cols, cols)]
-        gather_lanes(top, jnp.where(row == 6, part, 0.0), s * (each // 2), each // 2, each // 2, 0)
-    fc = fcs[0:1, :]
-    gather_lanes(top, jnp.where(wide_row == 7, fc, 0.0), 0, each, 2 * each, 0)
-    gather_lanes(low, jnp.where(wide_row == 0, fc, 0.0), 0, each, 2 * each, each)
     out_y.wait_recv()
     out_t.start()
     if direct:
         s_s.begin()
-        s_q[0].add(3)
-        s_q[0].add(0)
+        s_q[0].total()
+        s_q[1].total()
         for s in order:
-            s_q[1].add(s)
+            s_s.add(s)
         s_o.final(write_to(ro))
         results = [load(ro, ro_o)]
+        s_q[2].total()
         s_f.final(write_to(rf))
         results.append(load(rf, rf_o))
-        for s in order:
-            s_s.add(s)
-        for s in order:
-            s_q[2].add(s)
         s_s.total()
-        for p in range(n_pairs):
-            s_q[p].total()
     tok_y.wait_recv()
     tok_t.start()
     if direct:

time: 211 us -> 204 us (0.967)
  Pallas kernels: 210 us -> 203 us
    pallas_call x3, Pallas kernels: 210 us -> 203 us  [call(): pl.pallas_call(body, out_shape=[jax.ShapeDtypeStruct(s, t) for s, t in ou...]
where the time goes in v5:
time: 204 us
  Pallas kernels  203 us (100%)
    pallas_call x3, Pallas kernels, call(): pl.pallas_call(body, out_shape=[jax.ShapeDtypeStruct(s, t) for s, t in ou...  203 us

profile of v5, /device:TPU:0, one launch (start us, length us, event | category | flops | bytes accessed | tf_op | source)
XLA Modules:
  0.0 203.9 jit_solution(5074047905881790777)
XLA Ops:
  0.7 85.5 %forward.1 = (f32[8,768]{1,0:T(8,128)}, bf16[1024,768]{1,0:T(8,128)(2,1)}, bf16[768,1024]{1,0:T(8,128)(2,1)}, bf16[1024,768]{1,0:T(8,128)(2,1)}, bf16[768,1024]{...) custom-call(s32[2]{0:T(128)} %length.1, ...), custom_call_target="tpu_custom_call" | custom-call | tf_op jit(solution)/shard_map/forward/pallas_call | solution.py:960
  86.1 112.1 %backward.1 = (bf16[2,512,768]{2,1,0:T(8,128)(2,1)}, bf16[2,512,768]{2,1,0:T(8,128)(2,1)}, f32[16,128]{1,0:T(8,128)}, f32[3,96,384]{2,1,0:T(8,128)}, f32[96,384]...) custom-call(f32[8,768]{1,0:T(8,128)} %get-tuple-element.55.vec, bf16[1024,768]{1,0:T(8,128)(2,1)} %get-tuple-element.56.g_i, ...), custom_call_target="tpu_custom_call" | custom-call | tf_op jit(solution)/shard_map/backward/pallas_call | solution.py:960
  198.2 5.5 %finish.1 = (bf16[2,512,768]{2,1,0:T(8,128)(2,1)}, bf16[2,512,768]{2,1,0:T(8,128)(2,1)}, f32[3,96,384]{2,1,0:T(8,128)}, f32[96,384]{1,0:T(8,128)}, f32[96,1536]{...) custom-call(f32[16,128]{1,0:T(8,128)} %get-tuple-element.75.small, ...), custom_call_target="tpu_custom_call" | custom-call | tf_op jit(solution)/shard_map/finish/pallas_call | solution.py:960

commit v6 on v5

--- a/solution.py
+++ b/solution.py
@@ -294,8 +294,6 @@
     own(x, x_o)
     own(h1t, h1t_o)
     if direct:
-        for s in range(me.n_o):
-            st_o.cross(s)
         st_f.begin_inner()
         for s in (0, 2, 1) if n_s == 3 else range(n_s):
             st_f.relay(s)
@@ -317,11 +315,6 @@
     own(wq_v, wq_o)
     for src, dst in ((q, q_o), (k, k_o), (v, v_o), (kt, kt_o)):
         own(src, dst)
-    if direct:
-        for s in range(me.n_o):
-            st_f.cross(s)
-        cot_y.wait_recv()
-        cot_t.start()
 
     live = lax.broadcasted_iota(jnp.int32, (rows, step), 0) < live_length
     side = lax.broadcasted_iota(jnp.int32, (step, 128), 1) // HD
@@ -339,11 +332,38 @@
         p, j = it // n_blocks, it % n_blocks
         pair, at, slot = block(p, 128), block(j, step), it % 2
         if direct:
-            for s in range(n_s):
-
-                @pl.when(it == 2 + 3 * s if n_s == 3 else it == 2)
-                def _():
-                    st_p.relay(s)
+
+            @pl.when(it == 0)
+            def _():
+                for s in range(me.n_o):
+                    st_o.cross(s)
+                st_f.cross(0)
+
+            @pl.when(it == 1)
+            def _():
+                st_f.cross(1)
+                cot_y.wait_recv()
+                cot_t.start()
+
+            @pl.when(it == 2)
+            def _():
+                st_f.cross(3)
+
+            @pl.when(it == 3)
+            def _():
+                st_f.cross(2)
+
+            @pl.when(it == 4)
+            def _():
+                st_p.relay(0)
+
+            @pl.when(it == 8)
+            def _():
+                st_p.relay(1)
+
+            @pl.when(it == 11)
+            def _():
+                st_p.relay(2)
 
         @pl.when(it >= 2)
         def _():

time: 204 us -> 198 us (0.971)
  Pallas kernels: 203 us -> 197 us
    pallas_call x3, Pallas kernels: 203 us -> 197 us  [call(): pl.pallas_call(body, out_shape=[jax.ShapeDtypeStruct(s, t) for s, t in ou...]
where the time goes in v6:
time: 198 us
  Pallas kernels  197 us (99%)
    pallas_call x3, Pallas kernels, call(): pl.pallas_call(body, out_shape=[jax.ShapeDtypeStruct(s, t) for s, t in ou...  197 us

profile of v6, /device:TPU:0, one launch (start us, length us, event | category | flops | bytes accessed | tf_op | source)
XLA Modules:
  0.0 198.1 jit_solution(1011533466394296322)
XLA Ops:
  0.7 83.4 %forward.1 = (f32[8,768]{1,0:T(8,128)}, bf16[1024,768]{1,0:T(8,128)(2,1)}, bf16[768,1024]{1,0:T(8,128)(2,1)}, bf16[1024,768]{1,0:T(8,128)(2,1)}, bf16[768,1024]{...) custom-call(s32[2]{0:T(128)} %length.1, ...), custom_call_target="tpu_custom_call" | custom-call | tf_op jit(solution)/shard_map/forward/pallas_call | solution.py:980
  84.1 108.4 %backward.1 = (bf16[2,512,768]{2,1,0:T(8,128)(2,1)}, bf16[2,512,768]{2,1,0:T(8,128)(2,1)}, f32[16,128]{1,0:T(8,128)}, f32[3,96,384]{2,1,0:T(8,128)}, f32[96,384]...) custom-call(f32[8,768]{1,0:T(8,128)} %get-tuple-element.55.vec, bf16[1024,768]{1,0:T(8,128)(2,1)} %get-tuple-element.56.g_i, ...), custom_call_target="tpu_custom_call" | custom-call | tf_op jit(solution)/shard_map/backward/pallas_call | solution.py:980
  192.4 5.5 %finish.1 = (bf16[2,512,768]{2,1,0:T(8,128)(2,1)}, bf16[2,512,768]{2,1,0:T(8,128)(2,1)}, f32[3,96,384]{2,1,0:T(8,128)}, f32[96,384]{1,0:T(8,128)}, f32[96,1536]{...) custom-call(f32[16,128]{1,0:T(8,128)} %get-tuple-element.75.small, ...), custom_call_target="tpu_custom_call" | custom-call | tf_op jit(solution)/shard_map/finish/pallas_call | solution.py:980
